TPU v7x, 128 devices: a whole 4x4x4 slice. The times are simulated.
128 devices in a mesh: req: 8 (over z_lo, y), blk: 16 (over x, z_hi, core).
Axes of the slice: x: 4, y: 4, z: 4 (z_hi: 2, z_lo: 2; z = z_hi * 2 + z_lo), core: 2. Of those that a mesh axis runs over, the one named last changes fastest.
Arguments:
- hyper_state: float32 [128, 4, 2048], P(('req', 'blk')), may hold values from -6 to 6
- lengths: int32 [128], P('req'), may hold values from 1 to 16384
- key_cache: bfloat16 [128, 16, 2052, 128], P('req', 'blk'), may hold values from -360 to 360
- value_cache: bfloat16 [128, 16, 2052, 128], P('req', 'blk'), may hold values from -6 to 6
- attn_in_weight: bfloat16 [3, 2048, 2048], P(None, None, 'blk'), may hold values from -0.125 to 0.125
- attn_out_weight: bfloat16 [2048, 2048], P('blk'), may hold values from -0.125 to 0.125
- w_gate: bfloat16 [2048, 8192], P('req', 'blk'), may hold values from -0.125 to 0.125
- w_up: bfloat16 [2048, 8192], P('req', 'blk'), may hold values from -0.125 to 0.125
- w_down: bfloat16 [8192, 2048], P('blk', 'req'), may hold values from -0.0625 to 0.0625
- width_in: float32 [2, 4], replicated, may hold values from 0.2 to 1
- stream_mix: float32 [2, 4, 4], replicated, may hold values from -0.6 to 0.6
- depth_out: float32 [2, 4], replicated, may hold values from 0.5 to 1.5
Outputs:
- hyper_out: float32 [128, 4, 2048], P(('req', 'blk'))
All inputs are finite; a program needn't handle non-finite values.
Results may differ from a plain program's by a relative error of at most 0.023.
Values may be sent and summed in bfloat16 or wider, within the bound.
No kernel may reach another device: no remote copies, remote signals or barrier semaphores. Data moves between devices by JAX's collectives and lax.ppermute only.
A program may use at most 128 MiB of HBM per device.

v0:
```python
import math

import jax
import jax.numpy as jnp
from jax import lax
from jax.sharding import PartitionSpec as P


def layer_norm(values):
    center = values - jnp.mean(values, axis=-1, keepdims=True)
    spread = jnp.mean(center * center, axis=-1, keepdims=True)
    return center * lax.rsqrt(spread + 1e-05)


def combine(state, weights):
    return jnp.sum(state * weights[None, :, None], axis=1)


def remix(state, matrix):
    return jnp.sum(state[:, :, None, :] * matrix[None, :, :, None], axis=1)


def rotate(values, positions):
    half = values.shape[-1] // 2
    index = jnp.arange(half).astype(jnp.float32)
    freqs = jnp.exp(index * (-2.0 * math.log(10000.0) / values.shape[-1]))
    angles = positions.astype(jnp.float32)[:, None, None] * freqs[None, None, :]
    cosine = jnp.cos(angles)
    sine = jnp.sin(angles)
    first = values[..., :half]
    second = values[..., half:]
    return jnp.concatenate(
        [first * cosine - second * sine, second * cosine + first * sine], axis=-1
    )


def attend_group(query, key_new, value_new, keys, values, lengths):
    scale = query.shape[-1] ** (-0.5)
    scores = jnp.einsum("rhe,rhse->rhs", query, keys, preferred_element_type=jnp.float32) * scale
    own = jnp.sum(query.astype(jnp.float32) * key_new.astype(jnp.float32), axis=-1) * scale
    valid = jnp.arange(keys.shape[2])[None, None, :] < lengths[:, None, None]
    peak = jnp.maximum(jnp.max(jnp.where(valid, scores, -jnp.inf), axis=-1), own)
    shares = jnp.where(valid, jnp.exp(scores - peak[..., None]), 0.0)
    own_share = jnp.exp(own - peak)
    denom = jnp.sum(shares, axis=-1) + own_share
    probs = (shares / denom[..., None]).astype(jnp.bfloat16)
    own_prob = (own_share / denom).astype(jnp.bfloat16)
    mixed = jnp.einsum("rhs,rhse->rhe", probs, values, preferred_element_type=jnp.float32)
    mixed = mixed + own_prob.astype(jnp.float32)[..., None] * value_new.astype(jnp.float32)
    return mixed.astype(jnp.bfloat16)


def on_device(
    hyper_state,
    lengths,
    key_cache,
    value_cache,
    attn_in_weight,
    attn_out_weight,
    w_gate,
    w_up,
    w_down,
    width_in,
    stream_mix,
    depth_out,
):
    rows_here = hyper_state.shape[0]
    heads_here = key_cache.shape[1]
    head_size = key_cache.shape[3]
    normed = layer_norm(combine(hyper_state, width_in[0])).astype(jnp.bfloat16)
    projected = jnp.einsum(
        "rd,kde->rke",
        lax.all_gather(normed, "blk", axis=0, tiled=True),
        attn_in_weight,
        preferred_element_type=jnp.float32,
    )
    group = projected.shape[0]
    query = rotate(projected[:, 0].reshape(group, heads_here, head_size), lengths).astype(
        jnp.bfloat16
    )
    key_new = rotate(projected[:, 1].reshape(group, heads_here, head_size), lengths).astype(
        jnp.bfloat16
    )
    value_new = projected[:, 2].reshape(group, heads_here, head_size).astype(jnp.bfloat16)
    attended = attend_group(query, key_new, value_new, key_cache, value_cache, lengths)
    flat = attended.reshape(group, heads_here * head_size)
    attn_out = lax.psum_scatter(
        jnp.dot(flat, attn_out_weight, preferred_element_type=jnp.float32),
        "blk",
        scatter_dimension=0,
        tiled=True,
    )
    state = remix(hyper_state, stream_mix[0]) + depth_out[0][None, :, None] * attn_out[:, None, :]
    normed_mlp = layer_norm(combine(state, width_in[1])).astype(jnp.bfloat16)
    everyone = lax.all_gather(normed_mlp, ("req", "blk"), axis=0, tiled=True)
    feature_part = w_gate.shape[0]
    columns = lax.dynamic_slice_in_dim(
        everyone, lax.axis_index("req") * feature_part, feature_part, 1
    )
    gate_part = jnp.dot(columns, w_gate, preferred_element_type=jnp.float32)
    upward_part = jnp.dot(columns, w_up, preferred_element_type=jnp.float32)
    gate, upward = (
        lax.psum_scatter(gate_part, "req", scatter_dimension=0, tiled=True),
        lax.psum_scatter(upward_part, "req", scatter_dimension=0, tiled=True),
    )
    hidden = (jax.nn.silu(gate) * upward).astype(jnp.bfloat16)
    hidden_all = lax.all_gather(hidden, "req", axis=0, tiled=True)
    down_cols = jnp.dot(hidden_all, w_down, preferred_element_type=jnp.float32)
    req_count = lax.axis_size("req")
    blk_count = lax.axis_size("blk")
    column_part = w_down.shape[1]
    ordered = down_cols.reshape(req_count, blk_count, rows_here, column_part)
    ordered = jnp.transpose(ordered, (1, 0, 2, 3)).reshape(
        blk_count * req_count * rows_here, column_part
    )
    summed = lax.psum_scatter(ordered, "blk", scatter_dimension=0, tiled=True)
    mlp_out = lax.all_to_all(summed, "req", split_axis=0, concat_axis=1, tiled=True)
    return remix(state, stream_mix[1]) + depth_out[1][None, :, None] * mlp_out[:, None, :]


def solution(mesh):
    placed = (
        P(("req", "blk"), None, None),
        P("req"),
        P("req", "blk", None, None),
        P("req", "blk", None, None),
        P(None, None, "blk"),
        P("blk", None),
        P("req", "blk"),
        P("req", "blk"),
        P("blk", "req"),
        P(),
        P(),
        P(),
    )
    return jax.shard_map(
        on_device,
        mesh=mesh,
        in_specs=placed,
        out_specs=P(("req", "blk"), None, None),
        check_vma=False,
    )
```

profile of v0, /device:TPU:1, one launch (start us, length us, event | category | flops | bytes accessed | tf_op | source)
XLA Modules:
  0.0 544.9 jit_solution(18056339182733970401)
XLA Ops:
  6.5 0.9 slice_bitcast_fusion.2
  7.4 1.4 multiply_reduce_fusion.2
  9.5 0.6 multiply_reduce_fusion.6
  10.8 26.5 %all-gather = bf16[32768]{0:T(1024)(128)(2,1)S(1)} all-gather(bf16[2048]{0:T(1024)(128)(2,1)S(1)} %multiply_convert_fusion.2), channel_id=2, replica_groups=mesh['req'=8,'blk'=16] {'blk'}, dimensions={0}, use_global_device_ids=true | all-gather | bytes 69632 | tf_op jit(solution)/shard_map/all_gather | solution.py:73
  37.4 0.8 convert_element_type.116
  38.7 8.1 %fusion.2 = f32[16,1,2052]{2,1,0:T(1,128)S(1)} fusion(bf16[16,2052,128]{2,0,1:T(8,128)(2,1)} %bitcast.66, bf16[16,128,1]{1,0,2:T(8,128)(2,1)S(1)} %maximum_bitcast_fusion), kind=kOutput, calls=%fused_computation.2 | convolution fusion | flops 8404992 | bytes 8540416 | tf_op jit(solution)/shard_map/rhe,rhse->rhs/dot_general | solution.py:39
  47.6 4.4 fusion
  52.1 0.9 fusion.32
  53.8 132.2 %all-reduce.3.cloned.1.call-done = f32[16,2048]{1,0:T(8,128)} async-done(((f32[16,2048]{1,0:T(8,128)}), f32[16,2048]{1,0:T(8,128)}) %all-reduce.3.cloned.1.call-update) | async-done | bytes 131088
  185.9 1.5 constant_dynamic-slice_fusion
  187.4 0.7 fusion.12
  190.1 174.9 %all-gather.1 = bf16[262144]{0:T(1024)(128)(2,1)S(1)} all-gather(bf16[2048]{0:T(1024)(128)(2,1)S(1)} %multiply_convert_fusion.1), channel_id=3, replica_groups=mesh['req'=8,'blk'=16] {'req','blk'}, dimensions={0}, use_global_device_ids=true | all-gather | bytes 528384 | tf_op jit(solution)/shard_map/all_gather | solution.py:95
  365.2 0.9 fusion.7
  366.2 0.9 fusion.9
  367.2 24.4 %reduce-scatter.6.cloned.1.call-done = f32[16,512]{1,0:T(8,128)} async-done(((f32[128,512]{1,0:T(8,128)}), f32[16,512]{1,0:T(8,128)}) %reduce-scatter.6.cloned.1.call-update) | async-done | bytes 32784 | tf_op jit(solution)/shard_map/reduce_scatter | solution.py:104
  391.6 38.4 %reduce-scatter.4.cloned.1.call-done = f32[16,512]{1,0:T(8,128)} async-done(((f32[128,512]{1,0:T(8,128)}), f32[16,512]{1,0:T(8,128)}) %reduce-scatter.4.cloned.1.call-update) | async-done | bytes 32784 | tf_op jit(solution)/shard_map/reduce_scatter | solution.py:103
  430.0 0.8 multiply_convert_fusion
  430.8 21.8 %all_gather.11 = bf16[128,512]{1,0:T(8,128)(2,1)S(1)} all-gather(bf16[16,512]{1,0:T(8,128)(2,1)S(1)} %multiply_convert_fusion), channel_id=1, replica_groups=mesh['req'=8,'blk'=16] {'req'}, dimensions={0}, use_global_device_ids=true | all-gather | bytes 147456 | tf_op jit(solution)/shard_map/all_gather | solution.py:107
  452.8 0.7 copy.44
  453.6 73.6 %reduce-scatter.8.cloned.1.call-done = f32[8,256]{1,0:T(8,128)} async-done(((f32[128,256]{1,0:T(8,128)}), f32[8,256]{1,0:T(8,128)}) %reduce-scatter.8.cloned.1.call-update) | async-done | bytes 8208 | tf_op jit(solution)/shard_map/reduce_scatter | solution.py:116
  527.2 1.3 copy.17
  528.5 4.1 all-to-all-start
  532.7 4.9 all-to-all-done
  537.7 0.7 bitcast_add_fusion.1
  (49 shorter events, 3.5 us)
Async XLA Ops:
  6.5 31.6 %copy-start = (bf16[3,2048,128]{2,1,0:T(8,128)(2,1)S(1)}, bf16[3,2048,128]{2,1,0:T(8,128)(2,1)}, u32[]{:S(2)}) copy-start(bf16[3,2048,128]{2,1,0:T(8,128)(2,1)} %param.16) | copy-start | bytes 4718596
  6.5 40.2 %copy-start.6 = (s32[16]{0:T(128)S(1)}, s32[16]{0:T(128)}, u32[]{:S(2)}) copy-start(s32[16]{0:T(128)} %param.13) | copy-start | bytes 196
  6.5 179.4 %all-reduce.3.cloned.1.call-start = ((), (), s32[]{:S(2)}) async-start(), calls=%async_computation.7 | async-start | bytes 262144
  37.4 10.2 %copy-start.8 = (bf16[16,1,2052,128]{3,0,2,1:T(8,128)(2,1)S(1)}, bf16[16,1,2052,128]{3,0,2,1:T(8,128)(2,1)}, u32[]{:S(2)}) copy-start(bf16[16,1,2052,128]{3,0,2,1:T(8,128)(2,1)} %param.15) | copy-start | bytes 25214980
  46.8 5.3 copy-start.1
  46.8 6.3 %copy-start.7 = (f32[2,4,4]{2,1,0:T(4,128)S(1)}, f32[2,4,4]{2,1,0:T(4,128)}, u32[]{:S(2)}) copy-start(f32[2,4,4]{2,1,0:T(4,128)} %param.22) | copy-start | bytes 388
  46.8 6.3 %copy-start.9 = (u32[128]{0:T(128)S(1)}, u32[128]{0:T(128)}, u32[]{:S(2)}) copy-start(u32[128]{0:T(128)} %constant.43) | copy-start | bytes 1540
  46.8 6.9 %copy-start.5 = (f32[1,4,2048]{2,1,0:T(4,128)S(1)}, f32[1,4,2048]{2,1,0:T(4,128)}, u32[]{:S(2)}) copy-start(f32[1,4,2048]{2,1,0:T(4,128)} %param.12) | copy-start | bytes 98308
  46.8 318.4 %copy-start.3 = (bf16[256,512]{1,0:T(8,128)(2,1)S(1)}, bf16[256,512]{1,0:T(8,128)(2,1)}, u32[]{:S(2)}) copy-start(bf16[256,512]{1,0:T(8,128)(2,1)} %param.19) | copy-start | bytes 786436
  47.6 318.6 %copy-start.4 = (bf16[256,512]{1,0:T(8,128)(2,1)S(1)}, bf16[256,512]{1,0:T(8,128)(2,1)}, u32[]{:S(2)}) copy-start(bf16[256,512]{1,0:T(8,128)(2,1)} %param.18) | copy-start | bytes 786436
  47.6 405.0 %copy-start.2 = (bf16[512,256]{1,0:T(8,128)(2,1)S(1)}, bf16[512,256]{1,0:T(8,128)(2,1)}, u32[]{:S(2)}) copy-start(bf16[512,256]{1,0:T(8,128)(2,1)} %param.20) | copy-start | bytes 786436
  53.0 338.6 %reduce-scatter.6.cloned.1.call-start = ((), (), s32[]{:S(2)}) async-start(), calls=%async_computation.5 | async-start | bytes 294912 | tf_op jit(solution)/shard_map/reduce_scatter | solution.py:104
  366.2 63.8 %reduce-scatter.4.cloned.1.call-start = ((), (), s32[]{:S(2)}) async-start(), calls=%async_computation.4 | async-start | bytes 294912 | tf_op jit(solution)/shard_map/reduce_scatter | solution.py:103
  367.1 160.1 %reduce-scatter.8.cloned.1.call-start = ((), (), s32[]{:S(2)}) async-start(), calls=%async_computation.6 | async-start | bytes 139264 | tf_op jit(solution)/shard_map/reduce_scatter | solution.py:116
  528.5 9.1 %all-to-all-start = ((f32[8,1,256]{2,1,0:T(1,128)}), f32[8,1,256]{2,1,0:T(1,128)S(1)}, u32[]{:S(2)}, u32[]{:S(2)}) async-start(f32[8,1,256]{2,1,0:T(1,128)} %copy.17), calls=%async_computation.3 | async-start | bytes 16384 | tf_op jit(solution)/shard_map/all_to_all | solution.py:117
Sparse Core Ops, SparseCore 0:
  53.1 132.7 all-reduce.2
  366.3 25.2 reduce-scatter.5
  394.0 35.9 reduce-scatter.3
  453.7 73.5 reduce-scatter.7
where the time goes:
time: 548 us; the launch traced here: 545 us
  waiting for transfers between devices  274 us (50%)
  blocking collectives  223 us (41%)
  between operations  16 us (3%)
  matrix products  15.7 us (3%)
  other arithmetic  6.9 us (1%)
    all_gather x1, blocking collectives, on_device(): everyone = lax.all_gather(normed_mlp, ('req', 'blk'), axis=0, tiled=True)  175 us
    unnamed x5, waiting for transfers between devices  132 us
    reduce_scatter x1, waiting for transfers between devices, on_device(): summed = lax.psum_scatter(ordered, 'blk', scatter_dimension=0, tiled=True)  73.6 us
    reduce_scatter x1, waiting for transfers between devices, on_device(): lax.psum_scatter(gate_part, 'req', scatter_dimension=0, tiled=True)  38.4 us
    all_gather x1, blocking collectives, on_device(): lax.all_gather(normed, 'blk', axis=0, tiled=True)  26.5 us
    reduce_scatter x1, waiting for transfers between devices, on_device(): lax.psum_scatter(upward_part, 'req', scatter_dimension=0, tiled=True)  24.4 us
    all_gather x1, blocking collectives, on_device(): hidden_all = lax.all_gather(hidden, 'req', axis=0, tiled=True)  21.8 us
  transfers between devices with their start and end apart: 5, of which 5 were waited for; matrix products, arithmetic and copies ran while one was open for 0% of the time, Pallas kernels for 0%

commit v1 on v0

--- a/solution.py
+++ b/solution.py
@@ -50,6 +50,11 @@
     return mixed.astype(jnp.bfloat16)
 
 
+def spread(rows, axis):
+    copies = jnp.broadcast_to(rows[None], (lax.axis_size(axis),) + rows.shape)
+    return lax.all_to_all(copies, axis, split_axis=0, concat_axis=0, tiled=True)
+
+
 def on_device(
     hyper_state,
     lengths,
@@ -64,15 +69,16 @@
     stream_mix,
     depth_out,
 ):
-    rows_here = hyper_state.shape[0]
     heads_here = key_cache.shape[1]
     head_size = key_cache.shape[3]
+    width = hyper_state.shape[2]
+    req_count = lax.axis_size("req")
+    blk_count = lax.axis_size("blk")
+    both = ("req", "blk")
     normed = layer_norm(combine(hyper_state, width_in[0])).astype(jnp.bfloat16)
+    group_rows = spread(normed, "blk").reshape(blk_count, width)
     projected = jnp.einsum(
-        "rd,kde->rke",
-        lax.all_gather(normed, "blk", axis=0, tiled=True),
-        attn_in_weight,
-        preferred_element_type=jnp.float32,
+        "rd,kde->rke", group_rows, attn_in_weight, preferred_element_type=jnp.float32
     )
     group = projected.shape[0]
     query = rotate(projected[:, 0].reshape(group, heads_here, head_size), lengths).astype(
@@ -84,37 +90,38 @@
     value_new = projected[:, 2].reshape(group, heads_here, head_size).astype(jnp.bfloat16)
     attended = attend_group(query, key_new, value_new, key_cache, value_cache, lengths)
     flat = attended.reshape(group, heads_here * head_size)
-    attn_out = lax.psum_scatter(
-        jnp.dot(flat, attn_out_weight, preferred_element_type=jnp.float32),
-        "blk",
-        scatter_dimension=0,
-        tiled=True,
+    attn_part = jnp.dot(flat, attn_out_weight, preferred_element_type=jnp.float32)
+    attn_out = jnp.sum(
+        lax.all_to_all(attn_part, "blk", split_axis=0, concat_axis=0, tiled=True),
+        axis=0,
+        keepdims=True,
     )
     state = remix(hyper_state, stream_mix[0]) + depth_out[0][None, :, None] * attn_out[:, None, :]
     normed_mlp = layer_norm(combine(state, width_in[1])).astype(jnp.bfloat16)
-    everyone = lax.all_gather(normed_mlp, ("req", "blk"), axis=0, tiled=True)
     feature_part = w_gate.shape[0]
-    columns = lax.dynamic_slice_in_dim(
-        everyone, lax.axis_index("req") * feature_part, feature_part, 1
+    pieces = normed_mlp.reshape(req_count, 1, feature_part)
+    pieces = jnp.broadcast_to(pieces, (req_count, blk_count, feature_part))
+    columns = lax.all_to_all(
+        pieces.reshape(req_count * blk_count, feature_part),
+        both,
+        split_axis=0,
+        concat_axis=0,
+        tiled=True,
     )
+    hidden_part = w_gate.shape[1]
     gate_part = jnp.dot(columns, w_gate, preferred_element_type=jnp.float32)
-    upward_part = jnp.dot(columns, w_up, preferred_element_type=jnp.float32)
-    gate, upward = (
-        lax.psum_scatter(gate_part, "req", scatter_dimension=0, tiled=True),
-        lax.psum_scatter(upward_part, "req", scatter_dimension=0, tiled=True),
-    )
+    up_part = jnp.dot(columns, w_up, preferred_element_type=jnp.float32)
+    parts = jnp.concatenate([gate_part, up_part], axis=1).astype(jnp.bfloat16)
+    parts = parts.reshape(req_count, blk_count, 2 * hidden_part)
+    parts = lax.all_to_all(parts, "req", split_axis=0, concat_axis=0, tiled=True)
+    sums = jnp.sum(parts.astype(jnp.float32), axis=0)
+    gate = sums[:, :hidden_part]
+    upward = sums[:, hidden_part:]
     hidden = (jax.nn.silu(gate) * upward).astype(jnp.bfloat16)
-    hidden_all = lax.all_gather(hidden, "req", axis=0, tiled=True)
-    down_cols = jnp.dot(hidden_all, w_down, preferred_element_type=jnp.float32)
-    req_count = lax.axis_size("req")
-    blk_count = lax.axis_size("blk")
-    column_part = w_down.shape[1]
-    ordered = down_cols.reshape(req_count, blk_count, rows_here, column_part)
-    ordered = jnp.transpose(ordered, (1, 0, 2, 3)).reshape(
-        blk_count * req_count * rows_here, column_part
-    )
-    summed = lax.psum_scatter(ordered, "blk", scatter_dimension=0, tiled=True)
-    mlp_out = lax.all_to_all(summed, "req", split_axis=0, concat_axis=1, tiled=True)
+    hidden_all = spread(hidden, "req").reshape(req_count * blk_count, hidden_part)
+    down_part = jnp.dot(hidden_all, w_down, preferred_element_type=jnp.float32)
+    down = lax.all_to_all(down_part, both, split_axis=0, concat_axis=0, tiled=True)
+    mlp_out = jnp.sum(down.reshape(req_count, blk_count, feature_part), axis=1).reshape(1, width)
     return remix(state, stream_mix[1]) + depth_out[1][None, :, None] * mlp_out[:, None, :]
 
 

time: 548 us -> 104 us (0.19)
  waiting for transfers between devices: 274 us -> 23.4 us
  blocking collectives: 223 us -> 31.6 us
  starting transfers between devices: 4.24 us -> 19.9 us
  between operations: 16 us -> 3.06 us
    all_gather x3 -> x0, blocking collectives: 223 us -> none  [the longest x1 175 us: on_device(): everyone = lax.all_gather(normed_mlp, ('req', 'blk'), axis=0, tiled=True)]
    reduce_scatter x3 -> x0, waiting for transfers between devices: 136 us -> none  [the longest x1 73.6 us: on_device(): summed = lax.psum_scatter(ordered, 'blk', scatter_dimension=0, tiled=True)]
    unnamed x5 -> x0, waiting for transfers between devices: 132 us -> none
    all_to_all x0 -> x3, blocking collectives: none -> 31.6 us  [the longest x1 14.8 us: on_device(): lax.all_to_all(pieces.reshape(req_count * blk_count, feature_part), both,...]
    all_to_all x1 -> x3, waiting for transfers between devices: 4.94 us -> 23.4 us  [the longest x1 9.75 us: on_device(): lax.all_to_all(down_part, both, split_axis=0, concat_axis=0, tiled=True)]
    all_to_all x1 -> x3, starting transfers between devices: 4.11 us -> 19.9 us  [the longest x1 9.13 us: spread(): return lax.all_to_all(copies, axis, split_axis=0, concat_axis=0, tiled=True)]
  transfers between devices with their start and end apart: 5 -> 3, of which waited for: 5 -> 3; matrix products, arithmetic and copies ran while one was open for 0% -> 2% of each run, Pallas kernels for 0% -> 0%
where the time goes in v1:
time: 104 us
  blocking collectives  31.6 us (30%)
  waiting for transfers between devices  23.4 us (22%)
  starting transfers between devices  19.9 us (19%)
  matrix products  13.6 us (13%)
  other arithmetic  7.97 us (8%)
  local copies, waits for them, and re-layouts  4.52 us (4%)
  between operations  3.06 us (3%)
    all_to_all x1, blocking collectives, on_device(): lax.all_to_all(pieces.reshape(req_count * blk_count, feature_part), both,...  14.8 us
    all_to_all x1, waiting for transfers between devices, on_device(): lax.all_to_all(down_part, both, split_axis=0, concat_axis=0, tiled=True)  9.75 us
    all_to_all x1, starting transfers between devices, spread(): return lax.all_to_all(copies, axis, split_axis=0, concat_axis=0, tiled=True)  9.13 us
    all_to_all x1, blocking collectives, on_device(): lax.all_to_all(parts, 'req', split_axis=0, concat_axis=0, tiled=True)  8.85 us
    dot_general x1, matrix products, attend_group(): jnp.einsum('rhe,rhse->rhs', query, keys, preferred_element_type=jnp.float32)  8.04 us
    all_to_all x1, blocking collectives, spread(): return lax.all_to_all(copies, axis, split_axis=0, concat_axis=0, tiled=True)  7.91 us
    all_to_all x1, waiting for transfers between devices, on_device(): lax.all_to_all(attn_part, 'blk', split_axis=0, concat_axis=0, tiled=True)  7.6 us
    all_to_all x1, starting transfers between devices, on_device(): lax.all_to_all(down_part, both, split_axis=0, concat_axis=0, tiled=True)  7.07 us
  transfers between devices with their start and end apart: 3, of which 3 were waited for; matrix products, arithmetic and copies ran while one was open for 2% of the time, Pallas kernels for 0%

profile of v1, /device:TPU:1, one launch (start us, length us, event | category | flops | bytes accessed | tf_op | source)
XLA Modules:
  0.0 104.0 jit_solution(1766393516241553650)
XLA Ops:
  0.0 0.8 slice_bitcast_fusion.2
  0.8 1.4 %multiply_reduce_fusion.2 = (f32[]{:T(128)}, f32[2048]{0:T(1024)S(1)}) fusion(f32[1,4,2048]{2,1,0:T(4,128)} %param.12, f32[4]{0:T(128)S(1)} %get-tuple-element.20), kind=kLoop, calls=%fused_computation.31 | loop fusion | flops 22527 | bytes 40980 | tf_op jit(solution)/shard_map/reduce_sum | solution.py:10
  2.9 0.6 multiply_reduce_fusion.6
  4.8 1.0 reduce.18
  5.8 0.7 reshape.579
  6.5 9.1 %all-to-all-start = ((bf16[16,2,1024]{2,1,0:T(2,128)(2,1)}), bf16[16,2,1024]{2,1,0:T(2,128)(2,1)S(1)}, u32[]{:S(2)}, u32[]{:S(2)}) async-start(bf16[16,2,1024]{2,1,0:T(2,128)(2,1)} %reshape.579), calls=%async_computation | async-start | bytes 131072 | tf_op jit(solution)/shard_map/all_to_all | solution.py:55
  15.6 0.7 convert_element_type.113
  16.3 0.7 slice_bitcast_fusion.1
  17.0 6.0 %all-to-all-done = bf16[16,2,1024]{2,1,0:T(2,128)(2,1)S(1)} async-done(((bf16[16,2,1024]{2,1,0:T(2,128)(2,1)}), bf16[16,2,1024]{2,1,0:T(2,128)(2,1)S(1)}, u32[]{:S(2)}, u32[]{:S(2)}) %all-to-all-start) | async-done | bytes 65568 | tf_op jit(solution)/shard_map/all_to_all | solution.py:55
  23.6 8.0 %fusion.2 = f32[16,1,2052]{2,1,0:T(1,128)S(1)} fusion(bf16[16,2052,128]{2,0,1:T(8,128)(2,1)} %bitcast.74, bf16[16,128,1]{1,0,2:T(8,128)(2,1)S(1)} %maximum_bitcast_fusion), kind=kOutput, calls=%fused_computation.2 | convolution fusion | flops 8404992 | bytes 8540416 | tf_op jit(solution)/shard_map/rhe,rhse->rhs/dot_general | solution.py:39
  32.5 4.4 %fusion = f32[16,1,128]{2,1,0:T(1,128)S(1)} fusion(bf16[16,2052,128]{2,0,1:T(8,128)(2,1)S(1)} %bitcast.86, bf16[16,2052,1]{1,0,2:T(8,128)(2,1)S(1)} %fusion.8), kind=kOutput, calls=%fused_computation | convolution fusion | flops 8404992 | bytes 8478848 | tf_op jit(solution)/shard_map/rhs,rhse->rhe/dot_general | solution.py:48
  37.2 0.8 copy.18
  37.9 3.7 %all-to-all-start.1 = ((f32[16,1,2048]{2,1,0:T(1,128)}), f32[16,1,2048]{2,1,0:T(1,128)S(1)}, u32[]{:S(2)}, u32[]{:S(2)}) async-start(f32[16,1,2048]{2,1,0:T(1,128)} %copy.18), calls=%async_computation.1 | async-start | bytes 262144 | tf_op jit(solution)/shard_map/all_to_all | solution.py:95
  41.8 7.6 %all-to-all-done.1 = f32[16,1,2048]{2,1,0:T(1,128)S(1)} async-done(((f32[16,1,2048]{2,1,0:T(1,128)}), f32[16,1,2048]{2,1,0:T(1,128)S(1)}, u32[]{:S(2)}, u32[]{:S(2)}) %all-to-all-start.1) | async-done | bytes 131104 | tf_op jit(solution)/shard_map/all_to_all | solution.py:95
  49.5 0.8 fusion.14
  50.9 0.7 multiply_reduce_fusion.4
  52.4 0.7 reduce.19
  53.1 14.8 %all_to_all.42 = bf16[128,2,128]{2,1,0:T(2,128)(2,1)S(1)} all-to-all(bf16[128,2,128]{2,1,0:T(2,128)(2,1)S(1)} %reshape.581), channel_id=1, replica_groups=mesh['req'=8,'blk'=16] {'req','blk'}, dimensions={0} | all-to-all | bytes 131072 | tf_op jit(solution)/shard_map/all_to_all | solution.py:104
  68.4 8.8 %all_to_all.43 = bf16[8,16,1024]{2,1,0:T(8,128)(2,1)S(1)} all-to-all(bf16[8,16,1024]{2,1,0:T(8,128)(2,1)S(1)} %pad_maximum_fusion), channel_id=1, replica_groups=mesh['req'=8,'blk'=16] {'req'}, dimensions={0} | all-to-all | bytes 524288 | tf_op jit(solution)/shard_map/all_to_all | solution.py:116
  77.3 7.9 %all_to_all.44 = bf16[8,16,512]{2,1,0:T(8,128)(2,1)S(1)} all-to-all(bf16[8,16,512]{2,1,0:T(8,128)(2,1)S(1)} %broadcast_in_dim.17), channel_id=1, replica_groups=mesh['req'=8,'blk'=16] {'req'}, dimensions={0} | all-to-all | bytes 262144 | tf_op jit(solution)/shard_map/all_to_all | solution.py:55
  85.5 0.8 copy.20
  86.2 7.1 %all-to-all-start.5 = ((f32[128,1,256]{2,1,0:T(1,128)}), f32[128,1,256]{2,1,0:T(1,128)S(1)}, u32[]{:S(2)}, u32[]{:S(2)}) async-start(f32[128,1,256]{2,1,0:T(1,128)} %copy.20), calls=%async_computation.5 | async-start | bytes 262144 | tf_op jit(solution)/shard_map/all_to_all | solution.py:123
  93.5 9.8 %all-to-all-done.5 = f32[128,1,256]{2,1,0:T(1,128)S(1)} async-done(((f32[128,1,256]{2,1,0:T(1,128)}), f32[128,1,256]{2,1,0:T(1,128)S(1)}, u32[]{:S(2)}, u32[]{:S(2)}) %all-to-all-start.5) | async-done | bytes 131104 | tf_op jit(solution)/shard_map/all_to_all | solution.py:123
  103.3 0.7 bitcast_add_fusion.1
  (54 shorter events, 3.4 us)
Async XLA Ops:
  0.0 23.0 %copy-start = (bf16[3,2048,128]{2,1,0:T(8,128)(2,1)S(1)}, bf16[3,2048,128]{2,1,0:T(8,128)(2,1)}, u32[]{:S(2)}) copy-start(bf16[3,2048,128]{2,1,0:T(8,128)(2,1)} %param.16) | copy-start | bytes 4718596
  0.0 31.6 %copy-start.6 = (s32[16]{0:T(128)S(1)}, s32[16]{0:T(128)}, u32[]{:S(2)}) copy-start(s32[16]{0:T(128)} %param.13) | copy-start | bytes 196
  6.5 16.5 %all-to-all-start = ((bf16[16,2,1024]{2,1,0:T(2,128)(2,1)}), bf16[16,2,1024]{2,1,0:T(2,128)(2,1)S(1)}, u32[]{:S(2)}, u32[]{:S(2)}) async-start(bf16[16,2,1024]{2,1,0:T(2,128)(2,1)} %reshape.579), calls=%async_computation | async-start | bytes 131072 | tf_op jit(solution)/shard_map/all_to_all | solution.py:55
  23.0 9.4 %copy-start.8 = (bf16[16,1,2052,128]{3,0,2,1:T(8,128)(2,1)S(1)}, bf16[16,1,2052,128]{3,0,2,1:T(8,128)(2,1)}, u32[]{:S(2)}) copy-start(bf16[16,1,2052,128]{3,0,2,1:T(8,128)(2,1)} %param.15) | copy-start | bytes 25214980
  31.7 5.3 %copy-start.1 = (bf16[128,2048]{1,0:T(8,128)(2,1)S(1)}, bf16[128,2048]{1,0:T(8,128)(2,1)}, u32[]{:S(2)}) copy-start(bf16[128,2048]{1,0:T(8,128)(2,1)} %param.17) | copy-start | bytes 1572868
  31.7 10.0 %copy-start.7 = (f32[2,4]{1,0:T(2,128)S(1)}, f32[2,4]{1,0:T(2,128)}, u32[]{:S(2)}) copy-start(f32[2,4]{1,0:T(2,128)} %param.23) | copy-start | bytes 100
  31.7 10.0 %copy-start.5 = (f32[1,4,2048]{2,1,0:T(4,128)S(1)}, f32[1,4,2048]{2,1,0:T(4,128)}, u32[]{:S(2)}) copy-start(f32[1,4,2048]{2,1,0:T(4,128)} %param.12) | copy-start | bytes 98308
  31.7 36.3 %copy-start.2 = (bf16[256,512]{1,0:T(8,128)(2,1)S(1)}, bf16[256,512]{1,0:T(8,128)(2,1)}, u32[]{:S(2)}) copy-start(bf16[256,512]{1,0:T(8,128)(2,1)} %param.19) | copy-start | bytes 786436
  31.7 36.5 %copy-start.3 = (bf16[256,512]{1,0:T(8,128)(2,1)S(1)}, bf16[256,512]{1,0:T(8,128)(2,1)}, u32[]{:S(2)}) copy-start(bf16[256,512]{1,0:T(8,128)(2,1)} %param.18) | copy-start | bytes 786436
  32.5 52.8 %copy-start.4 = (bf16[512,256]{1,0:T(8,128)(2,1)S(1)}, bf16[512,256]{1,0:T(8,128)(2,1)}, u32[]{:S(2)}) copy-start(bf16[512,256]{1,0:T(8,128)(2,1)} %param.20) | copy-start | bytes 786436
  37.9 11.4 %all-to-all-start.1 = ((f32[16,1,2048]{2,1,0:T(1,128)}), f32[16,1,2048]{2,1,0:T(1,128)S(1)}, u32[]{:S(2)}, u32[]{:S(2)}) async-start(f32[16,1,2048]{2,1,0:T(1,128)} %copy.18), calls=%async_computation.1 | async-start | bytes 262144 | tf_op jit(solution)/shard_map/all_to_all | solution.py:95
  86.2 17.0 %all-to-all-start.5 = ((f32[128,1,256]{2,1,0:T(1,128)}), f32[128,1,256]{2,1,0:T(1,128)S(1)}, u32[]{:S(2)}, u32[]{:S(2)}) async-start(f32[128,1,256]{2,1,0:T(1,128)} %copy.20), calls=%async_computation.5 | async-start | bytes 262144 | tf_op jit(solution)/shard_map/all_to_all | solution.py:123

commit v2 on v0

v2 whole, which is shorter than its diff:
```python
import functools
import math

import jax
import jax.numpy as jnp
from jax import lax
from jax.experimental import pallas as pl
from jax.experimental.pallas import tpu as pltpu
from jax.sharding import Mesh, PartitionSpec as P

LANES = 128
FAR_BELOW = -1e30
VMEM = pl.BlockSpec(memory_space=pltpu.VMEM)
SMEM = pl.BlockSpec(memory_space=pltpu.SMEM)
HBM = pl.BlockSpec(memory_space=pl.ANY)


def normalize(values):
    count = values.shape[0] * values.shape[1]
    center = values - jnp.sum(values, keepdims=True) / count
    spread = jnp.sum(center * center, keepdims=True) / count
    return center * lax.rsqrt(spread + 1e-05)


def enter_kernel(state_ref, width_ref, mix_ref, send_ref, mixed_ref, tiles):
    streams, rows = tiles.shape[0], tiles.shape[1]
    for row in range(rows):
        tiles[:, row, :] = state_ref[0, :, row * LANES : (row + 1) * LANES]
    state = [tiles[stream] for stream in range(streams)]
    combined = sum(width_ref[0, stream] * state[stream] for stream in range(streams))
    send_ref[...] = jnp.broadcast_to(normalize(combined)[None], send_ref.shape)
    for target in range(streams):
        mixed_ref[target] = sum(mix_ref[0, stream, target] * state[stream] for stream in range(streams))


def halves_kernel(gate_hbm, up_hbm, down_hbm, own_ref, sent_ref, sems):
    half = own_ref.shape[1]
    side = lax.axis_index("zlo")
    copies = []
    for index, (target, which) in enumerate(((sent_ref, 1 - side), (own_ref, side))):
        begin = pl.multiple_of(which * half, half)
        copies += [
            pltpu.make_async_copy(gate_hbm.at[:, pl.ds(begin, half)], target.at[0], sems.at[3 * index]),
            pltpu.make_async_copy(up_hbm.at[:, pl.ds(begin, half)], target.at[1], sems.at[3 * index + 1]),
            pltpu.make_async_copy(down_hbm.at[pl.ds(begin, half), :], target.at[2], sems.at[3 * index + 2]),
        ]
    for copy in copies:
        copy.start()
    for copy in copies:
        copy.wait()


def attend_kernel(
    rows_ref,
    cos_ref,
    sin_ref,
    length_ref,
    weight_ref,
    keys_hbm,
    values_hbm,
    out_weight_ref,
    send_ref,
    keys,
    values,
    scores,
    key_sems,
    value_sems,
    *,
    pieces,
):
    def copies(source, target, sems):
        return [
            pltpu.make_async_copy(
                source.at[pl.ds(begin, size)], target.at[pl.ds(begin, size)], sems.at[index]
            )
            for index, (begin, size) in enumerate(pieces)
        ]

    key_copies = copies(keys_hbm, keys, key_sems)
    value_copies = copies(values_hbm, values, value_sems)
    for copy in key_copies + value_copies:
        copy.start()

    group = rows_ref.shape[0]
    head = keys.shape[1]
    rows = jnp.concatenate([rows_ref[:, row, :] for row in range(rows_ref.shape[1])], axis=1)
    rows = rows.astype(jnp.bfloat16)
    projected = [
        jnp.dot(rows, weight_ref[index], preferred_element_type=jnp.float32) for index in range(3)
    ]

    def rotate(part):
        turned = pltpu.roll(part, head // 2, 1)
        return (part * cos_ref[...] + turned * sin_ref[...]).astype(jnp.bfloat16)

    query = rotate(projected[0])
    key_new = rotate(projected[1])
    value_new = projected[2].astype(jnp.bfloat16)
    scale = head ** (-0.5)
    own = jnp.sum(
        query.astype(jnp.float32) * key_new.astype(jnp.float32), axis=1, keepdims=True
    )
    length = length_ref[...]
    peak = own
    for (begin, size), copy in zip(pieces, key_copies):
        copy.wait()
        part = lax.dot_general(
            query,
            keys[begin : begin + size, :],
            (((1,), (1,)), ((), ())),
            preferred_element_type=jnp.float32,
        )
        place = lax.broadcasted_iota(jnp.int32, part.shape, 1)
        mine = place % group == lax.broadcasted_iota(jnp.int32, part.shape, 0)
        inside = place < (length * group - begin)
        part = jnp.where(mine & inside, part, FAR_BELOW)
        scores[:, begin : begin + size] = part
        peak = jnp.maximum(peak, jnp.max(part, axis=1, keepdims=True))

    own_share = jnp.exp((own - peak) * scale)
    denom = own_share
    mixed = own_share * value_new.astype(jnp.float32)
    for (begin, size), copy in zip(pieces, value_copies):
        share = jnp.exp((scores[:, begin : begin + size] - peak) * scale)
        denom = denom + jnp.sum(share, axis=1, keepdims=True)
        copy.wait()
        mixed = mixed + jnp.dot(
            share.astype(jnp.bfloat16),
            values[begin : begin + size, :],
            preferred_element_type=jnp.float32,
        )
    attended = (mixed / denom).astype(jnp.bfloat16)
    part = jnp.dot(attended, out_weight_ref[...], preferred_element_type=jnp.float32)
    for row in range(send_ref.shape[1]):
        send_ref[:, row, :] = part[:, row * LANES : (row + 1) * LANES]


def middle_kernel(received_ref, mixed_ref, width_ref, mix_ref, depth_ref, send_ref, base_ref):
    streams = mixed_ref.shape[0]
    attn_out = jnp.sum(received_ref[...], axis=0)
    state = [mixed_ref[stream] + depth_ref[0, stream] * attn_out for stream in range(streams)]
    combined = sum(width_ref[1, stream] * state[stream] for stream in range(streams))
    normed = normalize(combined)
    half = normed.shape[0] // 2
    ring = lax.axis_size("y")
    step = half // ring
    shift = lax.rem((ring - lax.axis_index("y")) * step, half)
    first = pltpu.roll(normed[:half], shift, 0)
    second = pltpu.roll(normed[half:], shift, 0)
    count = send_ref.shape[0] // 2
    straight = jnp.concatenate([first, second], axis=0).astype(send_ref.dtype)
    crossed = jnp.concatenate([second, first], axis=0).astype(send_ref.dtype)
    shape = (count,) + straight.shape
    send_ref[:count] = jnp.broadcast_to(straight[None], shape)
    send_ref[count:] = jnp.broadcast_to(crossed[None], shape)
    for target in range(streams):
        base_ref[target] = sum(mix_ref[1, stream, target] * state[stream] for stream in range(streams))


def feed_kernel(received_ref, *refs):
    weight_refs, (send_ref, tiles) = refs[:-2], refs[-2:]
    tiles[...] = received_ref[...].astype(jnp.float32)
    part = weight_refs[0].shape[1]
    step = part // LANES
    gate = 0.0
    upward = 0.0
    for index, weight_ref in enumerate(weight_refs):
        piece = jnp.concatenate(
            [tiles[:, index * step + row, :] for row in range(step)], axis=1
        ).astype(jnp.bfloat16)
        gate = gate + jnp.dot(piece, weight_ref[0], preferred_element_type=jnp.float32)
        upward = upward + jnp.dot(piece, weight_ref[1], preferred_element_type=jnp.float32)
    hidden = (gate / (1.0 + jnp.exp(-gate)) * upward).astype(jnp.bfloat16)
    for index, weight_ref in enumerate(weight_refs):
        down = jnp.dot(hidden, weight_ref[2], preferred_element_type=jnp.float32)
        for row in range(step):
            tiles[:, index * step + row, :] = down[:, row * LANES : (row + 1) * LANES]
    send_ref[...] = tiles[...].astype(send_ref.dtype)


def leave_kernel(received_ref, base_ref, depth_ref, out_ref, tiles):
    count = received_ref.shape[0] // 2
    straight = jnp.sum(received_ref[:count].astype(jnp.float32), axis=0)
    crossed = jnp.sum(received_ref[count:].astype(jnp.float32), axis=0)
    half = straight.shape[0] // 2
    step = half // lax.axis_size("y")
    shift = lax.axis_index("y") * step
    first = pltpu.roll(straight[:half] + crossed[half:], shift, 0)
    second = pltpu.roll(straight[half:] + crossed[:half], shift, 0)
    mlp_out = jnp.concatenate([first, second], axis=0)
    for stream in range(tiles.shape[0]):
        tiles[stream] = base_ref[stream] + depth_ref[1, stream] * mlp_out
    for row in range(tiles.shape[1]):
        out_ref[0, :, row * LANES : (row + 1) * LANES] = tiles[:, row, :]


def turn_tables(lengths, head):
    half = head // 2
    index = jnp.arange(half).astype(jnp.float32)
    freqs = jnp.exp(index * (-2.0 * math.log(10000.0) / head))
    angles = lengths.astype(jnp.float32)[:, None] * freqs[None, :]
    cosine = jnp.cos(angles)
    sine = jnp.sin(angles)
    return (
        jnp.concatenate([cosine, cosine], axis=1),
        jnp.concatenate([-sine, sine], axis=1),
    )


def cut(total, size):
    return [(begin, min(size, total - begin)) for begin in range(0, total, size)]


def exchange(rows, axes):
    return lax.all_to_all(rows, axes, split_axis=0, concat_axis=0, tiled=True)


def on_device(
    hyper_state,
    lengths,
    key_cache,
    value_cache,
    attn_in_weight,
    attn_out_weight,
    w_gate,
    w_up,
    w_down,
    width_in,
    stream_mix,
    depth_out,
):
    streams, width = hyper_state.shape[1:]
    group, _, slots, head = key_cache.shape
    blk_count = lax.axis_size("blk")
    ring = lax.axis_size("y")
    plane = ("zlo", "blk")
    plane_count = lax.axis_size(plane)
    tiles = (width // LANES, LANES)
    f32, bf16 = jnp.float32, jnp.bfloat16

    half = w_gate.shape[1] // 2
    piece = jax.ShapeDtypeStruct((3, half, half), bf16)
    own, sent = pl.pallas_call(
        halves_kernel,
        out_shape=[piece, piece],
        in_specs=[HBM] * 3,
        out_specs=[HBM] * 2,
        scratch_shapes=[pltpu.SemaphoreType.DMA((6,))],
        name="halves",
    )(w_gate, w_up, w_down)

    def from_ahead(array, distance):
        return lax.ppermute(
            array, "y", [((place + distance) % ring, place) for place in range(ring)]
        )

    other = lax.ppermute(sent, "zlo", [(0, 1), (1, 0)])
    near = [own] + [from_ahead(own, distance) for distance in range(1, ring)]

    send, mixed = pl.pallas_call(
        enter_kernel,
        out_shape=[
            jax.ShapeDtypeStruct((blk_count,) + tiles, f32),
            jax.ShapeDtypeStruct((streams,) + tiles, f32),
        ],
        in_specs=[VMEM, SMEM, SMEM],
        out_specs=[VMEM] * 2,
        scratch_shapes=[pltpu.VMEM((streams,) + tiles, f32)],
        name="enter",
    )(hyper_state, width_in, stream_mix)
    group_rows = exchange(send, "blk")

    cosine, sine = turn_tables(lengths, head)
    in_cache_order = lambda cache: jnp.transpose(cache[:, 0], (1, 0, 2)).reshape(slots * group, head)
    pieces = cut(slots * group, 4096)
    send = pl.pallas_call(
        functools.partial(attend_kernel, pieces=pieces),
        out_shape=jax.ShapeDtypeStruct((group,) + tiles, f32),
        in_specs=[VMEM] * 5 + [HBM] * 2 + [VMEM],
        out_specs=VMEM,
        scratch_shapes=[
            pltpu.VMEM((slots * group, head), bf16),
            pltpu.VMEM((slots * group, head), bf16),
            pltpu.VMEM((group, slots * group), f32),
            pltpu.SemaphoreType.DMA((len(pieces),)),
            pltpu.SemaphoreType.DMA((len(pieces),)),
        ],
        compiler_params=pltpu.CompilerParams(vmem_limit_bytes=40 * 2**20),
        name="attend",
    )(
        group_rows,
        cosine,
        sine,
        lengths[:, None],
        attn_in_weight,
        in_cache_order(key_cache),
        in_cache_order(value_cache),
        attn_out_weight,
    )
    send, other = lax.optimization_barrier((send, other))
    far = [other] + [from_ahead(other, distance) for distance in range(1, ring)]
    received = exchange(send, "blk")

    send, base = pl.pallas_call(
        middle_kernel,
        out_shape=[
            jax.ShapeDtypeStruct((plane_count,) + tiles, bf16),
            jax.ShapeDtypeStruct((streams,) + tiles, f32),
        ],
        in_specs=[VMEM] * 2 + [SMEM] * 3,
        out_specs=[VMEM] * 2,
        name="middle",
    )(received, mixed, width_in, stream_mix, depth_out)
    received = exchange(send, plane)

    send = pl.pallas_call(
        feed_kernel,
        out_shape=jax.ShapeDtypeStruct((plane_count,) + tiles, bf16),
        in_specs=[VMEM] * (1 + 2 * ring),
        out_specs=VMEM,
        scratch_shapes=[pltpu.VMEM((plane_count,) + tiles, f32)],
        name="feed",
    )(received, *near, *far)
    received = exchange(send, plane)

    return pl.pallas_call(
        leave_kernel,
        out_shape=jax.ShapeDtypeStruct(hyper_state.shape, f32),
        in_specs=[VMEM] * 2 + [SMEM],
        out_specs=VMEM,
        scratch_shapes=[pltpu.VMEM((streams,) + tiles, f32)],
        name="leave",
    )(received, base, depth_out)


def solution(mesh):
    req_count = mesh.shape["req"]
    blk_count = mesh.shape["blk"]
    fine = Mesh(mesh.devices.reshape(2, req_count // 2, blk_count), ("zlo", "y", "blk"))
    req = ("zlo", "y")
    everyone = P(("zlo", "y", "blk"), None, None)
    placed = (
        everyone,
        P(req),
        P(req, "blk", None, None),
        P(req, "blk", None, None),
        P(None, None, "blk"),
        P("blk", None),
        P(req, "blk"),
        P(req, "blk"),
        P("blk", req),
        P(),
        P(),
        P(),
    )
    return jax.shard_map(
        on_device, mesh=fine, in_specs=placed, out_specs=everyone, check_vma=False
    )
```

time: 548 us -> 111 us (0.20)
  waiting for transfers between devices: 274 us -> 12.9 us
  blocking collectives: 223 us -> 24 us
  Pallas kernels: 0 us -> 41.3 us
  starting transfers between devices: 4.24 us -> 22.6 us
  between operations: 16 us -> 0.15 us
  matrix products: 15.7 us -> 0 us
  other arithmetic: 6.9 us -> 0.86 us
    all_gather x3 -> x0, blocking collectives: 223 us -> none  [the longest x1 175 us: on_device(): everyone = lax.all_gather(normed_mlp, ('req', 'blk'), axis=0, tiled=True)]
    reduce_scatter x3 -> x0, waiting for transfers between devices: 136 us -> none  [the longest x1 73.6 us: on_device(): summed = lax.psum_scatter(ordered, 'blk', scatter_dimension=0, tiled=True)]
    unnamed x5 -> x0, waiting for transfers between devices: 132 us -> none
    pallas_call x0 -> x6, Pallas kernels: none -> 41.3 us  [the longest x1 25 us: on_device(): pl.pallas_call(halves_kernel, out_shape=[piece, piece], in_specs=[HBM] *...]
    all_to_all x0 -> x2, blocking collectives: none -> 24 us  [exchange(): return lax.all_to_all(rows, axes, split_axis=0, concat_axis=0, tiled=True)]
    dot_general x7 -> x0, matrix products: 15.7 us -> none  [the longest x1 8.07 us: attend_group(): jnp.einsum('rhe,rhse->rhs', query, keys, preferred_element_type=jnp.float32)]
    ppermute x0 -> x7, starting transfers between devices: none -> 9.57 us  [the longest x6 8.84 us: from_ahead(): lax.ppermute(array, 'y', [((place + distance) % ring, place) for place in...]
    all_to_all x1 -> x2, starting transfers between devices: 4.11 us -> 13.1 us  [exchange(): return lax.all_to_all(rows, axes, split_axis=0, concat_axis=0, tiled=True)]
  transfers between devices with their start and end apart: 5 -> 9, of which waited for: 5 -> 2; matrix products, arithmetic and copies ran while one was open for 0% -> 1% of each run, Pallas kernels for 0% -> 10%
where the time goes in v2:
time: 111 us; the launch traced here: 110 us
  Pallas kernels  41.3 us (37%)
  blocking collectives  24 us (22%)
  starting transfers between devices  22.6 us (20%)
  waiting for transfers between devices  12.9 us (12%)
  local copies, waits for them, and re-layouts  8.22 us (7%)
    pallas_call x1, Pallas kernels, on_device(): pl.pallas_call(halves_kernel, out_shape=[piece, piece], in_specs=[HBM] *...  25 us
    all_to_all x2, blocking collectives, exchange(): return lax.all_to_all(rows, axes, split_axis=0, concat_axis=0, tiled=True)  24 us
    all_to_all x2, starting transfers between devices, exchange(): return lax.all_to_all(rows, axes, split_axis=0, concat_axis=0, tiled=True)  13.1 us
    all_to_all x2, waiting for transfers between devices, exchange(): return lax.all_to_all(rows, axes, split_axis=0, concat_axis=0, tiled=True)  12.9 us
    ppermute x6, starting transfers between devices, from_ahead(): lax.ppermute(array, 'y', [((place + distance) % ring, place) for place in...  8.84 us
    pallas_call x1, Pallas kernels, on_device(): pl.pallas_call(functools.partial(attend_kernel, pieces=pieces), out_shape...  7.82 us
    unnamed x22, local copies, waits for them, and re-layouts  7.48 us
    pallas_call x1, Pallas kernels, on_device(): pl.pallas_call(feed_kernel, out_shape=jax.ShapeDtypeStruct((plane_count,)...  3.28 us
  transfers between devices with their start and end apart: 9, of which 2 were waited for; matrix products, arithmetic and copies ran while one was open for 1% of the time, Pallas kernels for 10%

profile of v2, /device:TPU:1, one launch (start us, length us, event | category | flops | bytes accessed | tf_op | source)
XLA Modules:
  0.0 110.2 jit_solution(8401895015893766134)
XLA Ops:
  0.0 25.0 %halves.1 = (bf16[3,256,256]{2,1,0:T(8,128)(2,1)}, bf16[3,256,256]{2,1,0:T(8,128)(2,1)}) custom-call(bf16[256,512]{1,0:T(8,128)(2,1)} %gate_hbm.1, bf16[256,512]{1,0:T(8,128)(2,1)} %up_hbm.1, bf16[512,256]{1,0:T(8,128)(2,1)} %down_hbm.1), custom_call_target="tpu_custom_call" | custom-call | tf_op jit(solution)/shard_map/halves/pallas_call | solution.py:243
  25.0 2.2 %collective-permute-start.3 = (bf16[3,256,256]{2,1,0:T(8,128)(2,1)}, bf16[3,256,256]{2,1,0:T(8,128)(2,1)S(1)}, u32[]{:S(2)}, u32[]{:S(2)}) collective-permute-start(bf16[3,256,256]{2,1,0:T(8,128)(2,1)} %get-tuple-element.18.refs_0_), channel_id=1, source_target_pairs={{48,0},{0,16},{16,32},{32,48},{49,1},{1,17},{17,33},{33,49},{50,2}... | collective-permute-start | bytes 1179656 | tf_op jit(solution)/shard_map/ppermute | solution.py:253
  27.2 2.6 %collective-permute-start.2 = (bf16[3,256,256]{2,1,0:T(8,128)(2,1)}, bf16[3,256,256]{2,1,0:T(8,128)(2,1)S(1)}, u32[]{:S(2)}, u32[]{:S(2)}) collective-permute-start(bf16[3,256,256]{2,1,0:T(8,128)(2,1)} %get-tuple-element.18.refs_0_), channel_id=1, source_target_pairs={{32,0},{48,16},{0,32},{16,48},{33,1},{49,17},{1,33},{17,49},{34,2}... | collective-permute-start | bytes 1179656 | tf_op jit(solution)/shard_map/ppermute | solution.py:253
  29.8 1.1 collective-permute-start.1
  30.9 1.8 %enter.1 = (f32[16,16,128]{2,1,0:T(8,128)}, f32[4,16,128]{2,1,0:T(8,128)}) custom-call(f32[1,4,2048]{2,1,0:T(4,128)} %state_ref.1, f32[2,4]{1,0:T(2,128)} %width_ref.3, f32[2,4,4]{2,1,0:T(4,128)} %mix_ref.3), custom_call_target="tpu_custom_call" | custom-call | tf_op jit(solution)/shard_map/enter/pallas_call | solution.py:260
  32.7 9.1 %all-to-all-start = ((f32[16,16,128]{2,1,0:T(8,128)}), f32[16,16,128]{2,1,0:T(8,128)S(1)}, u32[]{:S(2)}, u32[]{:S(2)}) async-start(f32[16,16,128]{2,1,0:T(8,128)} %get-tuple-element.13), calls=%async_computation | async-start | bytes 262144 | tf_op jit(solution)/shard_map/all_to_all | solution.py:215
  41.8 0.7 collective-permute-start
  42.6 0.7 convert_element_type.10
  43.4 0.7 copy.13.length_ref
  44.2 5.3 %all-to-all-done.rows_ref = f32[16,16,128]{2,1,0:T(8,128)S(1)} async-done(((f32[16,16,128]{2,1,0:T(8,128)}), f32[16,16,128]{2,1,0:T(8,128)S(1)}, u32[]{:S(2)}, u32[]{:S(2)}) %all-to-all-start) | async-done | bytes 131104 | tf_op jit(solution)/shard_map/all_to_all | solution.py:215
  49.5 3.4 %copy-done = bf16[16,1,2052,128]{3,0,2,1:T(8,128)(2,1)S(1)} copy-done((bf16[16,1,2052,128]{3,0,2,1:T(8,128)(2,1)S(1)}, bf16[16,1,2052,128]{3,0,2,1:T(8,128)(2,1)}, u32[]{:S(2)}) %copy-start) | copy-done | bytes 8405016
  52.9 1.4 %copy-done.1 = bf16[3,2048,128]{2,1,0:T(8,128)(2,1)S(1)} copy-done((bf16[3,2048,128]{2,1,0:T(8,128)(2,1)S(1)}, bf16[3,2048,128]{2,1,0:T(8,128)(2,1)}, u32[]{:S(2)}) %copy-start.1) | copy-done | bytes 1572888
  54.3 1.0 copy-done.2
  55.4 7.8 %attend.1 = f32[16,16,128]{2,1,0:T(8,128)S(1)} custom-call(f32[16,16,128]{2,1,0:T(8,128)S(1)} %all-to-all-done.rows_ref, f32[16,128]{1,0:T(8,128)S(1)} %get-tuple-element.24.cos_ref, f32[16,128]{1,0:T(8,128)S(1)} %get-tuple-element.25.sin_ref, s32[16,1]{1,0:T(8,128)S(1)} %copy.13.length_ref, bf16[3,2048,128]{2,1,0:T(8,128)(2,1)S(1)} %copy-done.1, ...), custom_call_target="tpu_custom_call" | custom-call | tf_op jit(solution)/shard_map/attend/pallas_call | solution.py:276
  64.2 2.0 %collective-permute-start.4 = (bf16[3,256,256]{2,1,0:T(8,128)(2,1)S(1)}, bf16[3,256,256]{2,1,0:T(8,128)(2,1)S(1)}, u32[]{:S(2)}, u32[]{:S(2)}) collective-permute-start(bf16[3,256,256]{2,1,0:T(8,128)(2,1)S(1)} %collective-permute-done.refs_4_), channel_id=1, source_target_pairs={{16,0},{32,16},{48,32},{0,48},{17,1},{33,17},{49,33},{1,49},{18,2}... | collective-permute-start | bytes 1179656 | tf_op jit(solution)/shard_map/ppermute | solution.py:253
  66.2 11.7 %all_to_all.20.received_ref = f32[16,16,128]{2,1,0:T(8,128)} all-to-all(f32[16,16,128]{2,1,0:T(8,128)S(1)} %attend.1), channel_id=1, replica_groups=mesh['zlo'=2,'y'=4,'blk'=16] {'blk'}, dimensions={0} | all-to-all | bytes 262144 | tf_op jit(solution)/shard_map/all_to_all | solution.py:215
  77.9 1.9 %middle.1 = (bf16[32,16,128]{2,1,0:T(8,128)(2,1)}, f32[4,16,128]{2,1,0:T(8,128)}) custom-call(f32[16,16,128]{2,1,0:T(8,128)} %all_to_all.20.received_ref, f32[4,16,128]{2,1,0:T(8,128)} %get-tuple-element.16.mixed_ref, f32[2,4]{1,0:T(2,128)} %width_ref.3, f32[2,4,4]{2,1,0:T(4,128)} %mix_ref.3, f32[2,4]{1,0:T(2,128)} %depth_ref.3), custom_call_target="tpu_custom_call" | custom-call | tf_op jit(solution)/shard_map/middle/pallas_call | solution.py:304
  79.8 3.9 %all-to-all-start.2 = ((bf16[32,16,128]{2,1,0:T(8,128)(2,1)}), bf16[32,16,128]{2,1,0:T(8,128)(2,1)S(1)}, u32[]{:S(2)}, u32[]{:S(2)}) async-start(bf16[32,16,128]{2,1,0:T(8,128)(2,1)} %get-tuple-element.17), calls=%async_computation.2 | async-start | bytes 262144 | tf_op jit(solution)/shard_map/all_to_all | solution.py:215
  83.7 7.6 %all-to-all-done.2.received_ref = bf16[32,16,128]{2,1,0:T(8,128)(2,1)S(1)} async-done(((bf16[32,16,128]{2,1,0:T(8,128)(2,1)}), bf16[32,16,128]{2,1,0:T(8,128)(2,1)S(1)}, u32[]{:S(2)}, u32[]{:S(2)}) %all-to-all-start.2) | async-done | bytes 131104 | tf_op jit(solution)/shard_map/all_to_all | solution.py:215
  91.4 0.6 copy-done.3
  92.3 0.7 copy-done.10
  93.0 3.3 %feed.1 = bf16[32,16,128]{2,1,0:T(8,128)(2,1)} custom-call(bf16[32,16,128]{2,1,0:T(8,128)(2,1)} %copy-done.3, bf16[3,256,256]{2,1,0:T(8,128)(2,1)} %get-tuple-element.18.refs_0_, bf16[3,256,256]{2,1,0:T(8,128)(2,1)} %copy-done.6, bf16[3,256,256]{2,1,0:T(8,128)(2,1)} %copy-done.5, bf16[3,256,256]{2,1,0:T(8,128)(2,1)} %copy-done.4, ...), custom_call_target="tpu_custom_call" | custom-call | tf_op jit(solution)/shard_map/feed/pallas_call | solution.py:316
  96.3 12.3 %all_to_all.21.received_ref = bf16[32,16,128]{2,1,0:T(8,128)(2,1)} all-to-all(bf16[32,16,128]{2,1,0:T(8,128)(2,1)} %feed.1), channel_id=1, replica_groups=mesh['zlo'=2,'y'=4,'blk'=16] {'zlo','blk'}, dimensions={0} | all-to-all | bytes 262144 | tf_op jit(solution)/shard_map/all_to_all | solution.py:215
  108.6 1.6 %leave.1 = f32[1,4,2048]{2,1,0:T(4,128)} custom-call(bf16[32,16,128]{2,1,0:T(8,128)(2,1)} %all_to_all.21.received_ref, f32[4,16,128]{2,1,0:T(8,128)} %get-tuple-element.20.base_ref, f32[2,4]{1,0:T(2,128)} %depth_ref.3), custom_call_target="tpu_custom_call" | custom-call | tf_op jit(solution)/shard_map/leave/pallas_call | solution.py:326
  (29 shorter events, 1.5 us)
Async XLA Ops:
  25.0 39.2 %collective-permute-start.3 = (bf16[3,256,256]{2,1,0:T(8,128)(2,1)}, bf16[3,256,256]{2,1,0:T(8,128)(2,1)S(1)}, u32[]{:S(2)}, u32[]{:S(2)}) collective-permute-start(bf16[3,256,256]{2,1,0:T(8,128)(2,1)} %get-tuple-element.18.refs_0_), channel_id=1, source_target_pairs={{48,0},{0,16},{16,32},{32,48},{49,1},{1,17},{17,33},{33,49},{50,2}... | collective-permute-start | bytes 1179656 | tf_op jit(solution)/shard_map/ppermute | solution.py:253
  27.2 56.5 %collective-permute-start.2 = (bf16[3,256,256]{2,1,0:T(8,128)(2,1)}, bf16[3,256,256]{2,1,0:T(8,128)(2,1)S(1)}, u32[]{:S(2)}, u32[]{:S(2)}) collective-permute-start(bf16[3,256,256]{2,1,0:T(8,128)(2,1)} %get-tuple-element.18.refs_0_), channel_id=1, source_target_pairs={{32,0},{48,16},{0,32},{16,48},{33,1},{49,17},{1,33},{17,49},{34,2}... | collective-permute-start | bytes 1179656 | tf_op jit(solution)/shard_map/ppermute | solution.py:253
  29.8 53.9 %collective-permute-start.1 = (bf16[3,256,256]{2,1,0:T(8,128)(2,1)}, bf16[3,256,256]{2,1,0:T(8,128)(2,1)S(1)}, u32[]{:S(2)}, u32[]{:S(2)}) collective-permute-start(bf16[3,256,256]{2,1,0:T(8,128)(2,1)} %get-tuple-element.18.refs_0_), channel_id=1, source_target_pairs={{16,0},{32,16},{48,32},{0,48},{17,1},{33,17},{49,33},{1,49},{18,2}... | collective-permute-start | bytes 1179656 | tf_op jit(solution)/shard_map/ppermute | solution.py:253
  32.7 16.8 %all-to-all-start = ((f32[16,16,128]{2,1,0:T(8,128)}), f32[16,16,128]{2,1,0:T(8,128)S(1)}, u32[]{:S(2)}, u32[]{:S(2)}) async-start(f32[16,16,128]{2,1,0:T(8,128)} %get-tuple-element.13), calls=%async_computation | async-start | bytes 262144 | tf_op jit(solution)/shard_map/all_to_all | solution.py:215
  41.8 21.4 %collective-permute-start = (bf16[3,256,256]{2,1,0:T(8,128)(2,1)}, bf16[3,256,256]{2,1,0:T(8,128)(2,1)S(1)}, u32[]{:S(2)}, u32[]{:S(2)}) collective-permute-start(bf16[3,256,256]{2,1,0:T(8,128)(2,1)} %get-tuple-element.14), channel_id=1, source_target_pairs={{0,64},{64,0},{1,65},{65,1},{2,66},{66,2},{3,67},{67,3},{4,68},{68... | collective-permute-start | bytes 1179656 | tf_op jit(solution)/shard_map/ppermute | solution.py:257
  49.5 3.4 %copy-start = (bf16[16,1,2052,128]{3,0,2,1:T(8,128)(2,1)S(1)}, bf16[16,1,2052,128]{3,0,2,1:T(8,128)(2,1)}, u32[]{:S(2)}) copy-start(bf16[16,1,2052,128]{3,0,2,1:T(8,128)(2,1)} %param.14) | copy-start | bytes 25214980
  52.9 1.4 %copy-start.1 = (bf16[3,2048,128]{2,1,0:T(8,128)(2,1)S(1)}, bf16[3,2048,128]{2,1,0:T(8,128)(2,1)}, u32[]{:S(2)}) copy-start(bf16[3,2048,128]{2,1,0:T(8,128)(2,1)} %weight_ref.1) | copy-start | bytes 4718596
  54.3 1.0 copy-start.2
  63.2 28.2 %copy-start.7 = (bf16[3,256,256]{2,1,0:T(8,128)(2,1)}, bf16[3,256,256]{2,1,0:T(8,128)(2,1)S(1)}, u32[]{:S(2)}) copy-start(bf16[3,256,256]{2,1,0:T(8,128)(2,1)S(1)} %collective-permute-done.refs_4_) | copy-start | bytes 1179652
  63.2 28.1 %collective-permute-start.6 = (bf16[3,256,256]{2,1,0:T(8,128)(2,1)S(1)}, bf16[3,256,256]{2,1,0:T(8,128)(2,1)S(1)}, u32[]{:S(2)}, u32[]{:S(2)}) collective-permute-start(bf16[3,256,256]{2,1,0:T(8,128)(2,1)S(1)} %collective-permute-done.refs_4_), channel_id=1, source_target_pairs={{48,0},{0,16},{16,32},{32,48},{49,1},{1,17},{17,33},{33,49},{50,2}... | collective-permute-start | bytes 1179656 | tf_op jit(solution)/shard_map/ppermute | solution.py:253
  63.7 27.7 %collective-permute-start.5 = (bf16[3,256,256]{2,1,0:T(8,128)(2,1)S(1)}, bf16[3,256,256]{2,1,0:T(8,128)(2,1)S(1)}, u32[]{:S(2)}, u32[]{:S(2)}) collective-permute-start(bf16[3,256,256]{2,1,0:T(8,128)(2,1)S(1)} %collective-permute-done.refs_4_), channel_id=1, source_target_pairs={{32,0},{48,16},{0,32},{16,48},{33,1},{49,17},{1,33},{17,49},{34,2}... | collective-permute-start | bytes 1179656 | tf_op jit(solution)/shard_map/ppermute | solution.py:253
  64.2 27.2 %copy-start.4 = (bf16[3,256,256]{2,1,0:T(8,128)(2,1)}, bf16[3,256,256]{2,1,0:T(8,128)(2,1)S(1)}, u32[]{:S(2)}) copy-start(bf16[3,256,256]{2,1,0:T(8,128)(2,1)S(1)} %collective-permute-done.3.refs_3_) | copy-start | bytes 1179652
  64.2 27.2 %collective-permute-start.4 = (bf16[3,256,256]{2,1,0:T(8,128)(2,1)S(1)}, bf16[3,256,256]{2,1,0:T(8,128)(2,1)S(1)}, u32[]{:S(2)}, u32[]{:S(2)}) collective-permute-start(bf16[3,256,256]{2,1,0:T(8,128)(2,1)S(1)} %collective-permute-done.refs_4_), channel_id=1, source_target_pairs={{16,0},{32,16},{48,32},{0,48},{17,1},{33,17},{49,33},{1,49},{18,2}... | collective-permute-start | bytes 1179656 | tf_op jit(solution)/shard_map/ppermute | solution.py:253
  79.8 11.6 %all-to-all-start.2 = ((bf16[32,16,128]{2,1,0:T(8,128)(2,1)}), bf16[32,16,128]{2,1,0:T(8,128)(2,1)S(1)}, u32[]{:S(2)}, u32[]{:S(2)}) async-start(bf16[32,16,128]{2,1,0:T(8,128)(2,1)} %get-tuple-element.17), calls=%async_computation.2 | async-start | bytes 262144 | tf_op jit(solution)/shard_map/all_to_all | solution.py:215
  83.7 7.7 %copy-start.5 = (bf16[3,256,256]{2,1,0:T(8,128)(2,1)}, bf16[3,256,256]{2,1,0:T(8,128)(2,1)S(1)}, u32[]{:S(2)}) copy-start(bf16[3,256,256]{2,1,0:T(8,128)(2,1)S(1)} %collective-permute-done.2.refs_2_) | copy-start | bytes 1179652
  83.7 7.7 %copy-start.6 = (bf16[3,256,256]{2,1,0:T(8,128)(2,1)}, bf16[3,256,256]{2,1,0:T(8,128)(2,1)S(1)}, u32[]{:S(2)}) copy-start(bf16[3,256,256]{2,1,0:T(8,128)(2,1)S(1)} %collective-permute-done.1.refs_1_) | copy-start | bytes 1179652
  91.3 0.7 copy-start.3
  91.3 0.8 copy-start.8
  91.3 0.9 copy-start.9
  92.3 0.7 copy-start.10

commit v3 on v2

--- a/solution.py
+++ b/solution.py
@@ -12,7 +12,7 @@
 FAR_BELOW = -1e30
 VMEM = pl.BlockSpec(memory_space=pltpu.VMEM)
 SMEM = pl.BlockSpec(memory_space=pltpu.SMEM)
-HBM = pl.BlockSpec(memory_space=pl.ANY)
+HBM = pl.BlockSpec(memory_space=pltpu.HBM)
 
 
 def normalize(values):
@@ -22,18 +22,20 @@
     return center * lax.rsqrt(spread + 1e-05)
 
 
-def enter_kernel(state_ref, width_ref, mix_ref, send_ref, mixed_ref, tiles):
-    streams, rows = tiles.shape[0], tiles.shape[1]
-    for row in range(rows):
-        tiles[:, row, :] = state_ref[0, :, row * LANES : (row + 1) * LANES]
-    state = [tiles[stream] for stream in range(streams)]
-    combined = sum(width_ref[0, stream] * state[stream] for stream in range(streams))
-    send_ref[...] = jnp.broadcast_to(normalize(combined)[None], send_ref.shape)
-    for target in range(streams):
-        mixed_ref[target] = sum(mix_ref[0, stream, target] * state[stream] for stream in range(streams))
-
-
-def halves_kernel(gate_hbm, up_hbm, down_hbm, own_ref, sent_ref, sems):
+def enter_kernel(
+    state_ref,
+    gate_hbm,
+    up_hbm,
+    down_hbm,
+    width_ref,
+    mix_ref,
+    send_ref,
+    mixed_ref,
+    own_ref,
+    sent_ref,
+    tiles,
+    sems,
+):
     half = own_ref.shape[1]
     side = lax.axis_index("zlo")
     copies = []
@@ -46,23 +48,42 @@
         ]
     for copy in copies:
         copy.start()
+    streams, rows = tiles.shape[0], tiles.shape[1]
+    for row in range(rows):
+        tiles[:, row, :] = state_ref[0, :, row * LANES : (row + 1) * LANES]
+    state = [tiles[stream] for stream in range(streams)]
+    combined = sum(width_ref[0, stream] * state[stream] for stream in range(streams))
+    send_ref[...] = jnp.broadcast_to(normalize(combined)[None], send_ref.shape)
+    for target in range(streams):
+        mixed_ref[target] = sum(mix_ref[0, stream, target] * state[stream] for stream in range(streams))
     for copy in copies:
         copy.wait()
 
 
+def turn_tables(lengths):
+    head = lengths.shape[1]
+    place = lax.broadcasted_iota(jnp.int32, lengths.shape, 1)
+    index = (place % (head // 2)).astype(jnp.float32)
+    freqs = jnp.exp(index * (-2.0 * math.log(10000.0) / head))
+    angles = lengths.astype(jnp.float32) * freqs
+    sine = jnp.sin(angles)
+    return jnp.cos(angles), jnp.where(place < head // 2, -sine, sine)
+
+
 def attend_kernel(
     rows_ref,
-    cos_ref,
-    sin_ref,
     length_ref,
-    weight_ref,
+    weight_hbm,
     keys_hbm,
     values_hbm,
+    out_weight_hbm,
+    send_ref,
+    weight_ref,
     out_weight_ref,
-    send_ref,
     keys,
     values,
     scores,
+    weight_sems,
     key_sems,
     value_sems,
     *,
@@ -76,22 +97,30 @@
             for index, (begin, size) in enumerate(pieces)
         ]
 
+    weight_copy = pltpu.make_async_copy(weight_hbm, weight_ref, weight_sems.at[0])
+    out_weight_copy = pltpu.make_async_copy(out_weight_hbm, out_weight_ref, weight_sems.at[1])
     key_copies = copies(keys_hbm, keys, key_sems)
     value_copies = copies(values_hbm, values, value_sems)
-    for copy in key_copies + value_copies:
+    for copy in [weight_copy] + key_copies + value_copies + [out_weight_copy]:
         copy.start()
 
     group = rows_ref.shape[0]
     head = keys.shape[1]
+    request = lax.broadcasted_iota(jnp.int32, (group, head), 0)
+    lengths = jnp.zeros((group, head), jnp.int32)
+    for row in range(group):
+        lengths = jnp.where(request == row, length_ref[row], lengths)
+    cosine, sine = turn_tables(lengths)
     rows = jnp.concatenate([rows_ref[:, row, :] for row in range(rows_ref.shape[1])], axis=1)
     rows = rows.astype(jnp.bfloat16)
+    weight_copy.wait()
     projected = [
         jnp.dot(rows, weight_ref[index], preferred_element_type=jnp.float32) for index in range(3)
     ]
 
     def rotate(part):
         turned = pltpu.roll(part, head // 2, 1)
-        return (part * cos_ref[...] + turned * sin_ref[...]).astype(jnp.bfloat16)
+        return (part * cosine + turned * sine).astype(jnp.bfloat16)
 
     query = rotate(projected[0])
     key_new = rotate(projected[1])
@@ -100,7 +129,7 @@
     own = jnp.sum(
         query.astype(jnp.float32) * key_new.astype(jnp.float32), axis=1, keepdims=True
     )
-    length = length_ref[...]
+    length = lengths[:, :1]
     peak = own
     for (begin, size), copy in zip(pieces, key_copies):
         copy.wait()
@@ -130,6 +159,7 @@
             preferred_element_type=jnp.float32,
         )
     attended = (mixed / denom).astype(jnp.bfloat16)
+    out_weight_copy.wait()
     part = jnp.dot(attended, out_weight_ref[...], preferred_element_type=jnp.float32)
     for row in range(send_ref.shape[1]):
         send_ref[:, row, :] = part[:, row * LANES : (row + 1) * LANES]
@@ -143,8 +173,7 @@
     normed = normalize(combined)
     half = normed.shape[0] // 2
     ring = lax.axis_size("y")
-    step = half // ring
-    shift = lax.rem((ring - lax.axis_index("y")) * step, half)
+    shift = lax.rem((ring - lax.axis_index("y")) * (half // ring), half)
     first = pltpu.roll(normed[:half], shift, 0)
     second = pltpu.roll(normed[half:], shift, 0)
     count = send_ref.shape[0] // 2
@@ -158,23 +187,34 @@
 
 
 def feed_kernel(received_ref, *refs):
-    weight_refs, (send_ref, tiles) = refs[:-2], refs[-2:]
+    weight_hbms, (send_ref, weights, tiles, sems) = refs[:-4], refs[-4:]
+    ring = len(weight_hbms)
+    copies = [
+        pltpu.make_async_copy(weight_hbms[index], weights.at[index], sems.at[index])
+        for index in range(ring)
+    ]
+    for copy in copies:
+        copy.start()
     tiles[...] = received_ref[...].astype(jnp.float32)
-    part = weight_refs[0].shape[1]
-    step = part // LANES
+    step = weights.shape[3] // LANES
+    order = [(index, side) for index in range(ring) for side in range(2)]
     gate = 0.0
     upward = 0.0
-    for index, weight_ref in enumerate(weight_refs):
+    for index, side in order:
+        begin = (side * ring + index) * step
         piece = jnp.concatenate(
-            [tiles[:, index * step + row, :] for row in range(step)], axis=1
+            [tiles[:, begin + row, :] for row in range(step)], axis=1
         ).astype(jnp.bfloat16)
-        gate = gate + jnp.dot(piece, weight_ref[0], preferred_element_type=jnp.float32)
-        upward = upward + jnp.dot(piece, weight_ref[1], preferred_element_type=jnp.float32)
+        if side == 0:
+            copies[index].wait()
+        gate = gate + jnp.dot(piece, weights[index, side, 0], preferred_element_type=jnp.float32)
+        upward = upward + jnp.dot(piece, weights[index, side, 1], preferred_element_type=jnp.float32)
     hidden = (gate / (1.0 + jnp.exp(-gate)) * upward).astype(jnp.bfloat16)
-    for index, weight_ref in enumerate(weight_refs):
-        down = jnp.dot(hidden, weight_ref[2], preferred_element_type=jnp.float32)
+    for index, side in order:
+        begin = (side * ring + index) * step
+        down = jnp.dot(hidden, weights[index, side, 2], preferred_element_type=jnp.float32)
         for row in range(step):
-            tiles[:, index * step + row, :] = down[:, row * LANES : (row + 1) * LANES]
+            tiles[:, begin + row, :] = down[:, row * LANES : (row + 1) * LANES]
     send_ref[...] = tiles[...].astype(send_ref.dtype)
 
 
@@ -192,19 +232,6 @@
         tiles[stream] = base_ref[stream] + depth_ref[1, stream] * mlp_out
     for row in range(tiles.shape[1]):
         out_ref[0, :, row * LANES : (row + 1) * LANES] = tiles[:, row, :]
-
-
-def turn_tables(lengths, head):
-    half = head // 2
-    index = jnp.arange(half).astype(jnp.float32)
-    freqs = jnp.exp(index * (-2.0 * math.log(10000.0) / head))
-    angles = lengths.astype(jnp.float32)[:, None] * freqs[None, :]
-    cosine = jnp.cos(angles)
-    sine = jnp.sin(angles)
-    return (
-        jnp.concatenate([cosine, cosine], axis=1),
-        jnp.concatenate([-sine, sine], axis=1),
-    )
 
 
 def cut(total, size):
@@ -240,65 +267,56 @@
 
     half = w_gate.shape[1] // 2
     piece = jax.ShapeDtypeStruct((3, half, half), bf16)
-    own, sent = pl.pallas_call(
-        halves_kernel,
-        out_shape=[piece, piece],
-        in_specs=[HBM] * 3,
-        out_specs=[HBM] * 2,
-        scratch_shapes=[pltpu.SemaphoreType.DMA((6,))],
-        name="halves",
-    )(w_gate, w_up, w_down)
-
-    def from_ahead(array, distance):
-        return lax.ppermute(
-            array, "y", [((place + distance) % ring, place) for place in range(ring)]
-        )
-
-    other = lax.ppermute(sent, "zlo", [(0, 1), (1, 0)])
-    near = [own] + [from_ahead(own, distance) for distance in range(1, ring)]
-
-    send, mixed = pl.pallas_call(
+    send, mixed, own, sent = pl.pallas_call(
         enter_kernel,
         out_shape=[
             jax.ShapeDtypeStruct((blk_count,) + tiles, f32),
             jax.ShapeDtypeStruct((streams,) + tiles, f32),
+            piece,
+            piece,
         ],
-        in_specs=[VMEM, SMEM, SMEM],
-        out_specs=[VMEM] * 2,
-        scratch_shapes=[pltpu.VMEM((streams,) + tiles, f32)],
+        in_specs=[VMEM] + [HBM] * 3 + [SMEM] * 2,
+        out_specs=[VMEM] * 4,
+        scratch_shapes=[pltpu.VMEM((streams,) + tiles, f32), pltpu.SemaphoreType.DMA((6,))],
         name="enter",
-    )(hyper_state, width_in, stream_mix)
+    )(hyper_state, w_gate, w_up, w_down, width_in, stream_mix)
+
+    other = lax.ppermute(sent, "zlo", [(0, 1), (1, 0)])
+    both = jnp.stack([own, other])
+    weights = [both] + [
+        lax.ppermute(both, "y", [((place + distance) % ring, place) for place in range(ring)])
+        for distance in range(1, ring)
+    ]
     group_rows = exchange(send, "blk")
 
-    cosine, sine = turn_tables(lengths, head)
     in_cache_order = lambda cache: jnp.transpose(cache[:, 0], (1, 0, 2)).reshape(slots * group, head)
-    pieces = cut(slots * group, 4096)
+    pieces = cut(slots * group, 8192)
     send = pl.pallas_call(
         functools.partial(attend_kernel, pieces=pieces),
         out_shape=jax.ShapeDtypeStruct((group,) + tiles, f32),
-        in_specs=[VMEM] * 5 + [HBM] * 2 + [VMEM],
+        in_specs=[VMEM, SMEM] + [HBM] * 4,
         out_specs=VMEM,
         scratch_shapes=[
+            pltpu.VMEM(attn_in_weight.shape, bf16),
+            pltpu.VMEM(attn_out_weight.shape, bf16),
             pltpu.VMEM((slots * group, head), bf16),
             pltpu.VMEM((slots * group, head), bf16),
             pltpu.VMEM((group, slots * group), f32),
+            pltpu.SemaphoreType.DMA((2,)),
             pltpu.SemaphoreType.DMA((len(pieces),)),
             pltpu.SemaphoreType.DMA((len(pieces),)),
         ],
-        compiler_params=pltpu.CompilerParams(vmem_limit_bytes=40 * 2**20),
+        compiler_params=pltpu.CompilerParams(vmem_limit_bytes=63 * 2**20),
+        cost_estimate=pl.CostEstimate(flops=3 * 10**12, transcendentals=0, bytes_accessed=20 * 2**20),
         name="attend",
     )(
         group_rows,
-        cosine,
-        sine,
-        lengths[:, None],
+        lengths,
         attn_in_weight,
         in_cache_order(key_cache),
         in_cache_order(value_cache),
         attn_out_weight,
     )
-    send, other = lax.optimization_barrier((send, other))
-    far = [other] + [from_ahead(other, distance) for distance in range(1, ring)]
     received = exchange(send, "blk")
 
     send, base = pl.pallas_call(
@@ -316,11 +334,15 @@
     send = pl.pallas_call(
         feed_kernel,
         out_shape=jax.ShapeDtypeStruct((plane_count,) + tiles, bf16),
-        in_specs=[VMEM] * (1 + 2 * ring),
+        in_specs=[VMEM] + [HBM] * ring,
         out_specs=VMEM,
-        scratch_shapes=[pltpu.VMEM((plane_count,) + tiles, f32)],
+        scratch_shapes=[
+            pltpu.VMEM((ring,) + both.shape, bf16),
+            pltpu.VMEM((plane_count,) + tiles, f32),
+            pltpu.SemaphoreType.DMA((ring,)),
+        ],
         name="feed",
-    )(received, *near, *far)
+    )(received, *weights)
     received = exchange(send, plane)
 
     return pl.pallas_call(

time: 111 us -> 86 us (0.77)
  blocking collectives: 24 us -> 42.9 us
  Pallas kernels: 41.3 us -> 23.3 us
  waiting for transfers between devices: 12.9 us -> 0.84 us
  local copies, waits for them, and re-layouts: 8.22 us -> 0.65 us
  starting transfers between devices: 22.6 us -> 15.7 us
    pallas_call x1 -> x0, Pallas kernels: 25 us -> none  [on_device(): pl.pallas_call(halves_kernel, out_shape=[piece, piece], in_specs=[HBM] *...]
    all_to_all x2 -> x3, blocking collectives: 24 us -> 42.9 us  [exchange(): return lax.all_to_all(rows, axes, split_axis=0, concat_axis=0, tiled=True)]
    all_to_all x2 -> x1, waiting for transfers between devices: 12.9 us -> 0.09 us  [exchange(): return lax.all_to_all(rows, axes, split_axis=0, concat_axis=0, tiled=True)]
    unnamed x22 -> x2, local copies, waits for them, and re-layouts: 7.48 us -> 0.65 us
    pallas_call x1, Pallas kernels: 7.82 us -> 12.7 us  [on_device(): pl.pallas_call(functools.partial(attend_kernel, pieces=pieces), out_shape...]
    all_to_all x2 -> x1, starting transfers between devices: 13.1 us -> 8.29 us  [exchange(): return lax.all_to_all(rows, axes, split_axis=0, concat_axis=0, tiled=True)]
    ppermute x6 -> x3, starting transfers between devices: 8.84 us -> 4.89 us  [on_device(): lax.ppermute(both, 'y', [((place + distance) % ring, place) for place in...]
    another operation x0 -> x1, other arithmetic: none -> 1.95 us  [on_device(): both = jnp.stack([own, other])]
  transfers between devices with their start and end apart: 9 -> 5, of which waited for: 2 -> 2; matrix products, arithmetic and copies ran while one was open for 1% -> 2% of each run, Pallas kernels for 10% -> 17%
where the time goes in v3:
time: 86 us; the launch traced here: 85.4 us
  blocking collectives  42.9 us (50%)
  Pallas kernels  23.3 us (27%)
  starting transfers between devices  15.7 us (18%)
  other arithmetic  1.95 us (2%)
    all_to_all x3, blocking collectives, exchange(): return lax.all_to_all(rows, axes, split_axis=0, concat_axis=0, tiled=True)  42.9 us
    pallas_call x1, Pallas kernels, on_device(): pl.pallas_call(functools.partial(attend_kernel, pieces=pieces), out_shape...  12.7 us
    all_to_all x1, starting transfers between devices, exchange(): return lax.all_to_all(rows, axes, split_axis=0, concat_axis=0, tiled=True)  8.29 us
    ppermute x3, starting transfers between devices, on_device(): lax.ppermute(both, 'y', [((place + distance) % ring, place) for place in...  4.89 us
    pallas_call x1, Pallas kernels, on_device(): pl.pallas_call(feed_kernel, out_shape=jax.ShapeDtypeStruct((plane_count,)...  3.99 us
    pallas_call x1, Pallas kernels, on_device(): pl.pallas_call(enter_kernel, out_shape=[jax.ShapeDtypeStruct((blk_count,)...  3.15 us
    ppermute x1, starting transfers between devices, on_device(): other = lax.ppermute(sent, 'zlo', [(0, 1), (1, 0)])  2.55 us
    another operation x1, other arithmetic, on_device(): both = jnp.stack([own, other])  1.95 us
  transfers between devices with their start and end apart: 5, of which 2 were waited for; matrix products, arithmetic and copies ran while one was open for 2% of the time, Pallas kernels for 17%

profile of v3, /device:TPU:1, one launch (start us, length us, event | category | flops | bytes accessed | tf_op | source)
XLA Modules:
  0.0 85.4 jit_solution(12791237981174906452)
XLA Ops:
  0.0 3.1 %enter.1 = (f32[16,16,128]{2,1,0:T(8,128)}, f32[4,16,128]{2,1,0:T(8,128)}, bf16[3,256,256]{2,1,0:T(8,128)(2,1)}, bf16[3,256,256]{2,1,0:T(8,128)(2,1)}) custom-call(f32[1,4,2048]{2,1,0:T(4,128)} %state_ref.1, bf16[256,512]{1,0:T(8,128)(2,1)} %gate_hbm.1, bf16[256,512]{1,0:T(8,128)(2,1)} %up_hbm.1, bf16[512,256]{1,0:T(8,128)(2,1)} %down_hbm.1, ...), custom_call_target="tpu_custom_call" | custom-call | tf_op jit(solution)/shard_map/enter/pallas_call | solution.py:270
  3.2 2.5 %collective-permute-start = (bf16[3,256,256]{2,1,0:T(8,128)(2,1)}, bf16[3,256,256]{2,1,0:T(8,128)(2,1)S(1)}, u32[]{:S(2)}, u32[]{:S(2)}) collective-permute-start(bf16[3,256,256]{2,1,0:T(8,128)(2,1)} %get-tuple-element.15), channel_id=1, source_target_pairs={{0,64},{64,0},{1,65},{65,1},{2,66},{66,2},{3,67},{67,3},{4,68},{68... | collective-permute-start | bytes 1179656 | tf_op jit(solution)/shard_map/ppermute | solution.py:284
  5.7 8.3 %all-to-all-start = ((f32[16,16,128]{2,1,0:T(8,128)}), f32[16,16,128]{2,1,0:T(8,128)S(1)}, u32[]{:S(2)}, u32[]{:S(2)}) async-start(f32[16,16,128]{2,1,0:T(8,128)} %get-tuple-element.11), calls=%async_computation | async-start | bytes 262144 | tf_op jit(solution)/shard_map/all_to_all | solution.py:242
  14.0 0.7 collective-permute-done
  14.7 2.0 %pad_maximum_fusion.refs_0_ = bf16[2,3,256,256]{3,2,1,0:T(8,128)(2,1)} fusion(bf16[1,3,256,256]{3,2,1,0:T(8,128)(2,1)S(1)} %bitcast.13, bf16[1,3,256,256]{3,2,1,0:T(8,128)(2,1)} %bitcast.12), kind=kLoop, calls=%fused_computation | loop fusion | flops 393216 | bytes 1572864 | tf_op jit(solution)/shard_map/stack | solution.py:285
  16.7 1.2 %collective-permute-start.3 = (bf16[2,3,256,256]{3,2,1,0:T(8,128)(2,1)}, bf16[2,3,256,256]{3,2,1,0:T(8,128)(2,1)}, u32[]{:S(2)}, u32[]{:S(2)}) collective-permute-start(bf16[2,3,256,256]{3,2,1,0:T(8,128)(2,1)} %pad_maximum_fusion.refs_0_), channel_id=1, source_target_pairs={{48,0},{0,16},{16,32},{32,48},{49,1},{1,17},{17,33},{33,49},{50,2}... | collective-permute-start | bytes 2359304 | tf_op jit(solution)/shard_map/ppermute | solution.py:287
  17.9 2.6 %collective-permute-start.2 = (bf16[2,3,256,256]{3,2,1,0:T(8,128)(2,1)}, bf16[2,3,256,256]{3,2,1,0:T(8,128)(2,1)}, u32[]{:S(2)}, u32[]{:S(2)}) collective-permute-start(bf16[2,3,256,256]{3,2,1,0:T(8,128)(2,1)} %pad_maximum_fusion.refs_0_), channel_id=1, source_target_pairs={{32,0},{48,16},{0,32},{16,48},{33,1},{49,17},{1,33},{17,49},{34,2}... | collective-permute-start | bytes 2359304 | tf_op jit(solution)/shard_map/ppermute | solution.py:287
  20.5 1.1 %collective-permute-start.1 = (bf16[2,3,256,256]{3,2,1,0:T(8,128)(2,1)}, bf16[2,3,256,256]{3,2,1,0:T(8,128)(2,1)}, u32[]{:S(2)}, u32[]{:S(2)}) collective-permute-start(bf16[2,3,256,256]{3,2,1,0:T(8,128)(2,1)} %pad_maximum_fusion.refs_0_), channel_id=1, source_target_pairs={{16,0},{32,16},{48,32},{0,48},{17,1},{33,17},{49,33},{1,49},{18,2}... | collective-permute-start | bytes 2359304 | tf_op jit(solution)/shard_map/ppermute | solution.py:287
  21.6 0.1 all-to-all-done.rows_ref
  21.7 0.0 copy-start
  21.7 0.6 copy-done
  22.3 12.7 %attend.1 = f32[16,16,128]{2,1,0:T(8,128)} custom-call(f32[16,16,128]{2,1,0:T(8,128)} %copy-done, s32[16]{0:T(128)} %length_ref.1, bf16[3,2048,128]{2,1,0:T(8,128)(2,1)} %weight_hbm.1, bf16[32832,128]{1,0:T(8,128)(2,1)} %bitcast.14, bf16[32832,128]{1,0:T(8,128)(2,1)} %bitcast.15, bf16[128,2048]{1,0:T(8,128)(2,1)} %out_weight_hbm.1), custom_call_target="tpu_custom_call" | custom-call | flops 3000000053248 | bytes 20971520 | tf_op jit(solution)/shard_map/attend/pallas_call | solution.py:294
  35.0 18.5 %all_to_all.20.received_ref = f32[16,16,128]{2,1,0:T(8,128)} all-to-all(f32[16,16,128]{2,1,0:T(8,128)} %attend.1), channel_id=1, replica_groups=mesh['zlo'=2,'y'=4,'blk'=16] {'blk'}, dimensions={0} | all-to-all | bytes 262144 | tf_op jit(solution)/shard_map/all_to_all | solution.py:242
  53.5 1.9 %middle.1 = (bf16[32,16,128]{2,1,0:T(8,128)(2,1)}, f32[4,16,128]{2,1,0:T(8,128)}) custom-call(f32[16,16,128]{2,1,0:T(8,128)} %all_to_all.20.received_ref, f32[4,16,128]{2,1,0:T(8,128)} %get-tuple-element.12.mixed_ref, f32[2,4]{1,0:T(2,128)} %width_ref.3, f32[2,4,4]{2,1,0:T(4,128)} %mix_ref.3, f32[2,4]{1,0:T(2,128)} %depth_ref.3), custom_call_target="tpu_custom_call" | custom-call | tf_op jit(solution)/shard_map/middle/pallas_call | solution.py:322
  55.4 12.2 %all_to_all.21.received_ref = bf16[32,16,128]{2,1,0:T(8,128)(2,1)} all-to-all(bf16[32,16,128]{2,1,0:T(8,128)(2,1)} %get-tuple-element.13), channel_id=1, replica_groups=mesh['zlo'=2,'y'=4,'blk'=16] {'zlo','blk'}, dimensions={0} | all-to-all | bytes 262144 | tf_op jit(solution)/shard_map/all_to_all | solution.py:242
  67.5 0.0 collective-permute-done.3.refs_3_
  67.5 0.0 collective-permute-done.2.refs_2_
  67.5 0.0 collective-permute-done.1.refs_1_
  67.6 4.0 %feed.1 = bf16[32,16,128]{2,1,0:T(8,128)(2,1)} custom-call(bf16[32,16,128]{2,1,0:T(8,128)(2,1)} %all_to_all.21.received_ref, bf16[2,3,256,256]{3,2,1,0:T(8,128)(2,1)} %pad_maximum_fusion.refs_0_, bf16[2,3,256,256]{3,2,1,0:T(8,128)(2,1)} %collective-permute-done.1.refs_1_, bf16[2,3,256,256]{3,2,1,0:T(8,128)(2,1)} %collective-permute-done.2.refs_2_, ...), custom_call_target="tpu_custom_call" | custom-call | tf_op jit(solution)/shard_map/feed/pallas_call | solution.py:334
  71.5 12.3 %all_to_all.22.received_ref = bf16[32,16,128]{2,1,0:T(8,128)(2,1)} all-to-all(bf16[32,16,128]{2,1,0:T(8,128)(2,1)} %feed.1), channel_id=1, replica_groups=mesh['zlo'=2,'y'=4,'blk'=16] {'zlo','blk'}, dimensions={0} | all-to-all | bytes 262144 | tf_op jit(solution)/shard_map/all_to_all | solution.py:242
  83.8 1.6 %leave.1 = f32[1,4,2048]{2,1,0:T(4,128)} custom-call(bf16[32,16,128]{2,1,0:T(8,128)(2,1)} %all_to_all.22.received_ref, f32[4,16,128]{2,1,0:T(8,128)} %get-tuple-element.16.base_ref, f32[2,4]{1,0:T(2,128)} %depth_ref.3), custom_call_target="tpu_custom_call" | custom-call | tf_op jit(solution)/shard_map/leave/pallas_call | solution.py:348
Async XLA Ops:
  3.2 11.6 %collective-permute-start = (bf16[3,256,256]{2,1,0:T(8,128)(2,1)}, bf16[3,256,256]{2,1,0:T(8,128)(2,1)S(1)}, u32[]{:S(2)}, u32[]{:S(2)}) collective-permute-start(bf16[3,256,256]{2,1,0:T(8,128)(2,1)} %get-tuple-element.15), channel_id=1, source_target_pairs={{0,64},{64,0},{1,65},{65,1},{2,66},{66,2},{3,67},{67,3},{4,68},{68... | collective-permute-start | bytes 1179656 | tf_op jit(solution)/shard_map/ppermute | solution.py:284
  5.7 16.0 %all-to-all-start = ((f32[16,16,128]{2,1,0:T(8,128)}), f32[16,16,128]{2,1,0:T(8,128)S(1)}, u32[]{:S(2)}, u32[]{:S(2)}) async-start(f32[16,16,128]{2,1,0:T(8,128)} %get-tuple-element.11), calls=%async_computation | async-start | bytes 262144 | tf_op jit(solution)/shard_map/all_to_all | solution.py:242
  16.7 50.9 %collective-permute-start.3 = (bf16[2,3,256,256]{3,2,1,0:T(8,128)(2,1)}, bf16[2,3,256,256]{3,2,1,0:T(8,128)(2,1)}, u32[]{:S(2)}, u32[]{:S(2)}) collective-permute-start(bf16[2,3,256,256]{3,2,1,0:T(8,128)(2,1)} %pad_maximum_fusion.refs_0_), channel_id=1, source_target_pairs={{48,0},{0,16},{16,32},{32,48},{49,1},{1,17},{17,33},{33,49},{50,2}... | collective-permute-start | bytes 2359304 | tf_op jit(solution)/shard_map/ppermute | solution.py:287
  17.9 49.7 %collective-permute-start.2 = (bf16[2,3,256,256]{3,2,1,0:T(8,128)(2,1)}, bf16[2,3,256,256]{3,2,1,0:T(8,128)(2,1)}, u32[]{:S(2)}, u32[]{:S(2)}) collective-permute-start(bf16[2,3,256,256]{3,2,1,0:T(8,128)(2,1)} %pad_maximum_fusion.refs_0_), channel_id=1, source_target_pairs={{32,0},{48,16},{0,32},{16,48},{33,1},{49,17},{1,33},{17,49},{34,2}... | collective-permute-start | bytes 2359304 | tf_op jit(solution)/shard_map/ppermute | solution.py:287
  20.5 47.0 %collective-permute-start.1 = (bf16[2,3,256,256]{3,2,1,0:T(8,128)(2,1)}, bf16[2,3,256,256]{3,2,1,0:T(8,128)(2,1)}, u32[]{:S(2)}, u32[]{:S(2)}) collective-permute-start(bf16[2,3,256,256]{3,2,1,0:T(8,128)(2,1)} %pad_maximum_fusion.refs_0_), channel_id=1, source_target_pairs={{16,0},{32,16},{48,32},{0,48},{17,1},{33,17},{49,33},{1,49},{18,2}... | collective-permute-start | bytes 2359304 | tf_op jit(solution)/shard_map/ppermute | solution.py:287
  21.7 0.6 copy-start

commit v4 on v3

--- a/solution.py
+++ b/solution.py
@@ -10,6 +10,7 @@
 
 LANES = 128
 FAR_BELOW = -1e30
+DEPTH = 12
 VMEM = pl.BlockSpec(memory_space=pltpu.VMEM)
 SMEM = pl.BlockSpec(memory_space=pltpu.SMEM)
 HBM = pl.BlockSpec(memory_space=pltpu.HBM)
@@ -83,25 +84,31 @@
     keys,
     values,
     scores,
-    weight_sems,
-    key_sems,
-    value_sems,
+    sems,
     *,
     pieces,
+    steps,
 ):
-    def copies(source, target, sems):
-        return [
-            pltpu.make_async_copy(
-                source.at[pl.ds(begin, size)], target.at[pl.ds(begin, size)], sems.at[index]
+    queue = [pltpu.make_async_copy(weight_hbm, weight_ref, sems.at[0])]
+    for source, target in ((keys_hbm, keys), (values_hbm, values)):
+        for begin, size in pieces:
+            queue.append(
+                pltpu.make_async_copy(
+                    source.at[pl.ds(begin, size)],
+                    target.at[pl.ds(begin, size)],
+                    sems.at[len(queue)],
+                )
             )
-            for index, (begin, size) in enumerate(pieces)
-        ]
-
-    weight_copy = pltpu.make_async_copy(weight_hbm, weight_ref, weight_sems.at[0])
-    out_weight_copy = pltpu.make_async_copy(out_weight_hbm, out_weight_ref, weight_sems.at[1])
-    key_copies = copies(keys_hbm, keys, key_sems)
-    value_copies = copies(values_hbm, values, value_sems)
-    for copy in [weight_copy] + key_copies + value_copies + [out_weight_copy]:
+    queue.append(pltpu.make_async_copy(out_weight_hbm, out_weight_ref, sems.at[len(queue)]))
+    waited = iter(range(len(queue)))
+
+    def arrive():
+        index = next(waited)
+        queue[index].wait()
+        if index + DEPTH < len(queue):
+            queue[index + DEPTH].start()
+
+    for copy in queue[:DEPTH]:
         copy.start()
 
     group = rows_ref.shape[0]
@@ -113,7 +120,7 @@
     cosine, sine = turn_tables(lengths)
     rows = jnp.concatenate([rows_ref[:, row, :] for row in range(rows_ref.shape[1])], axis=1)
     rows = rows.astype(jnp.bfloat16)
-    weight_copy.wait()
+    arrive()
     projected = [
         jnp.dot(rows, weight_ref[index], preferred_element_type=jnp.float32) for index in range(3)
     ]
@@ -131,8 +138,13 @@
     )
     length = lengths[:, :1]
     peak = own
-    for (begin, size), copy in zip(pieces, key_copies):
-        copy.wait()
+
+    def within(begin, size):
+        return [piece for piece in pieces if begin <= piece[0] < begin + size]
+
+    for begin, size in steps:
+        for _ in within(begin, size):
+            arrive()
         part = lax.dot_general(
             query,
             keys[begin : begin + size, :],
@@ -149,17 +161,18 @@
     own_share = jnp.exp((own - peak) * scale)
     denom = own_share
     mixed = own_share * value_new.astype(jnp.float32)
-    for (begin, size), copy in zip(pieces, value_copies):
+    for begin, size in steps:
         share = jnp.exp((scores[:, begin : begin + size] - peak) * scale)
         denom = denom + jnp.sum(share, axis=1, keepdims=True)
-        copy.wait()
+        for _ in within(begin, size):
+            arrive()
         mixed = mixed + jnp.dot(
             share.astype(jnp.bfloat16),
             values[begin : begin + size, :],
             preferred_element_type=jnp.float32,
         )
     attended = (mixed / denom).astype(jnp.bfloat16)
-    out_weight_copy.wait()
+    arrive()
     part = jnp.dot(attended, out_weight_ref[...], preferred_element_type=jnp.float32)
     for row in range(send_ref.shape[1]):
         send_ref[:, row, :] = part[:, row * LANES : (row + 1) * LANES]
@@ -188,33 +201,28 @@
 
 def feed_kernel(received_ref, *refs):
     weight_hbms, (send_ref, weights, tiles, sems) = refs[:-4], refs[-4:]
-    ring = len(weight_hbms)
     copies = [
-        pltpu.make_async_copy(weight_hbms[index], weights.at[index], sems.at[index])
-        for index in range(ring)
+        pltpu.make_async_copy(source, weights.at[index], sems.at[index])
+        for index, source in enumerate(weight_hbms)
     ]
     for copy in copies:
         copy.start()
     tiles[...] = received_ref[...].astype(jnp.float32)
-    step = weights.shape[3] // LANES
-    order = [(index, side) for index in range(ring) for side in range(2)]
+    step = weights.shape[2] // LANES
     gate = 0.0
     upward = 0.0
-    for index, side in order:
-        begin = (side * ring + index) * step
+    for index, copy in enumerate(copies):
         piece = jnp.concatenate(
-            [tiles[:, begin + row, :] for row in range(step)], axis=1
+            [tiles[:, index * step + row, :] for row in range(step)], axis=1
         ).astype(jnp.bfloat16)
-        if side == 0:
-            copies[index].wait()
-        gate = gate + jnp.dot(piece, weights[index, side, 0], preferred_element_type=jnp.float32)
-        upward = upward + jnp.dot(piece, weights[index, side, 1], preferred_element_type=jnp.float32)
+        copy.wait()
+        gate = gate + jnp.dot(piece, weights[index, 0], preferred_element_type=jnp.float32)
+        upward = upward + jnp.dot(piece, weights[index, 1], preferred_element_type=jnp.float32)
     hidden = (gate / (1.0 + jnp.exp(-gate)) * upward).astype(jnp.bfloat16)
-    for index, side in order:
-        begin = (side * ring + index) * step
-        down = jnp.dot(hidden, weights[index, side, 2], preferred_element_type=jnp.float32)
+    for index in range(len(copies)):
+        down = jnp.dot(hidden, weights[index, 2], preferred_element_type=jnp.float32)
         for row in range(step):
-            tiles[:, begin + row, :] = down[:, row * LANES : (row + 1) * LANES]
+            tiles[:, index * step + row, :] = down[:, row * LANES : (row + 1) * LANES]
     send_ref[...] = tiles[...].astype(send_ref.dtype)
 
 
@@ -281,18 +289,21 @@
         name="enter",
     )(hyper_state, w_gate, w_up, w_down, width_in, stream_mix)
 
-    other = lax.ppermute(sent, "zlo", [(0, 1), (1, 0)])
-    both = jnp.stack([own, other])
-    weights = [both] + [
-        lax.ppermute(both, "y", [((place + distance) % ring, place) for place in range(ring)])
-        for distance in range(1, ring)
-    ]
+    def gathered(array):
+        return [array] + [
+            lax.ppermute(array, "y", [((place + distance) % ring, place) for place in range(ring)])
+            for distance in range(1, ring)
+        ]
+
+    near = gathered(own)
+    far = gathered(lax.ppermute(sent, "zlo", [(0, 1), (1, 0)]))
     group_rows = exchange(send, "blk")
 
     in_cache_order = lambda cache: jnp.transpose(cache[:, 0], (1, 0, 2)).reshape(slots * group, head)
-    pieces = cut(slots * group, 8192)
+    pieces = cut(slots * group, 4096)
+    steps = cut(slots * group, 8192)
     send = pl.pallas_call(
-        functools.partial(attend_kernel, pieces=pieces),
+        functools.partial(attend_kernel, pieces=pieces, steps=steps),
         out_shape=jax.ShapeDtypeStruct((group,) + tiles, f32),
         in_specs=[VMEM, SMEM] + [HBM] * 4,
         out_specs=VMEM,
@@ -302,9 +313,7 @@
             pltpu.VMEM((slots * group, head), bf16),
             pltpu.VMEM((slots * group, head), bf16),
             pltpu.VMEM((group, slots * group), f32),
-            pltpu.SemaphoreType.DMA((2,)),
-            pltpu.SemaphoreType.DMA((len(pieces),)),
-            pltpu.SemaphoreType.DMA((len(pieces),)),
+            pltpu.SemaphoreType.DMA((2 + 2 * len(pieces),)),
         ],
         compiler_params=pltpu.CompilerParams(vmem_limit_bytes=63 * 2**20),
         cost_estimate=pl.CostEstimate(flops=3 * 10**12, transcendentals=0, bytes_accessed=20 * 2**20),
@@ -318,6 +327,7 @@
         attn_out_weight,
     )
     received = exchange(send, "blk")
+    received, near = lax.optimization_barrier((received, near))
 
     send, base = pl.pallas_call(
         middle_kernel,
@@ -327,6 +337,7 @@
         ],
         in_specs=[VMEM] * 2 + [SMEM] * 3,
         out_specs=[VMEM] * 2,
+        cost_estimate=pl.CostEstimate(flops=2 * 10**9, transcendentals=0, bytes_accessed=2**20),
         name="middle",
     )(received, mixed, width_in, stream_mix, depth_out)
     received = exchange(send, plane)
@@ -334,15 +345,15 @@
     send = pl.pallas_call(
         feed_kernel,
         out_shape=jax.ShapeDtypeStruct((plane_count,) + tiles, bf16),
-        in_specs=[VMEM] + [HBM] * ring,
+        in_specs=[VMEM] + [HBM] * (2 * ring),
         out_specs=VMEM,
         scratch_shapes=[
-            pltpu.VMEM((ring,) + both.shape, bf16),
+            pltpu.VMEM((2 * ring,) + own.shape, bf16),
             pltpu.VMEM((plane_count,) + tiles, f32),
-            pltpu.SemaphoreType.DMA((ring,)),
+            pltpu.SemaphoreType.DMA((2 * ring,)),
         ],
         name="feed",
-    )(received, *weights)
+    )(received, *near, *far)
     received = exchange(send, plane)
 
     return pl.pallas_call(

time: 86 us -> 81 us (0.942)
  blocking collectives: 42.9 us -> 27.3 us
  waiting for transfers between devices: 0.84 us -> 8.22 us
  starting transfers between devices: 15.7 us -> 22.9 us
  Pallas kernels: 23.3 us -> 19.8 us
  other arithmetic: 1.95 us -> 0 us
  local copies, waits for them, and re-layouts: 0.65 us -> 2.07 us
    all_to_all x3 -> x2, blocking collectives: 42.9 us -> 27.3 us  [exchange(): return lax.all_to_all(rows, axes, split_axis=0, concat_axis=0, tiled=True)]
    all_to_all x1 -> x2, waiting for transfers between devices: 0.09 us -> 7.34 us  [exchange(): return lax.all_to_all(rows, axes, split_axis=0, concat_axis=0, tiled=True)]
    all_to_all x1 -> x2, starting transfers between devices: 8.29 us -> 14.9 us  [exchange(): return lax.all_to_all(rows, axes, split_axis=0, concat_axis=0, tiled=True)]
    pallas_call x1, Pallas kernels: 12.7 us -> 9.3 us  [on_device(): pl.pallas_call(functools.partial(attend_kernel, pieces=pieces, steps=step...]
    another operation x1 -> x0, other arithmetic: 1.95 us -> none  [on_device(): both = jnp.stack([own, other])]
    unnamed x2 -> x10, local copies, waits for them, and re-layouts: 0.65 us -> 2.07 us
    ppermute x4 -> x7, starting transfers between devices: 7.43 us -> 8 us  [the longest x6 7.27 us: gathered(): lax.ppermute(array, 'y', [((place + distance) % ring, place) for place in...]
  transfers between devices with their start and end apart: 5 -> 9, of which waited for: 2 -> 3; matrix products, arithmetic and copies ran while one was open for 2% -> 0% of each run, Pallas kernels for 17% -> 14%
where the time goes in v4:
time: 81 us; the launch traced here: 80.4 us
  blocking collectives  27.3 us (34%)
  starting transfers between devices  22.9 us (28%)
  Pallas kernels  19.8 us (24%)
  waiting for transfers between devices  8.22 us (10%)
  local copies, waits for them, and re-layouts  2.07 us (3%)
    all_to_all x2, blocking collectives, exchange(): return lax.all_to_all(rows, axes, split_axis=0, concat_axis=0, tiled=True)  27.3 us
    all_to_all x2, starting transfers between devices, exchange(): return lax.all_to_all(rows, axes, split_axis=0, concat_axis=0, tiled=True)  14.9 us
    pallas_call x1, Pallas kernels, on_device(): pl.pallas_call(functools.partial(attend_kernel, pieces=pieces, steps=step...  9.3 us
    all_to_all x2, waiting for transfers between devices, exchange(): return lax.all_to_all(rows, axes, split_axis=0, concat_axis=0, tiled=True)  7.34 us
    ppermute x6, starting transfers between devices, gathered(): lax.ppermute(array, 'y', [((place + distance) % ring, place) for place in...  7.27 us
    pallas_call x1, Pallas kernels, on_device(): pl.pallas_call(feed_kernel, out_shape=jax.ShapeDtypeStruct((plane_count,)...  3.92 us
    pallas_call x1, Pallas kernels, on_device(): pl.pallas_call(enter_kernel, out_shape=[jax.ShapeDtypeStruct((blk_count,)...  3.16 us
    unnamed x10, local copies, waits for them, and re-layouts  2.07 us
  transfers between devices with their start and end apart: 9, of which 3 were waited for; matrix products, arithmetic and copies ran while one was open for 0% of the time, Pallas kernels for 14%

profile of v4, /device:TPU:1, one launch (start us, length us, event | category | flops | bytes accessed | tf_op | source)
XLA Modules:
  0.0 80.4 jit_solution(17023833586564449072)
XLA Ops:
  0.0 3.2 %enter.1 = (f32[16,16,128]{2,1,0:T(8,128)}, f32[4,16,128]{2,1,0:T(8,128)}, bf16[3,256,256]{2,1,0:T(8,128)(2,1)}, bf16[3,256,256]{2,1,0:T(8,128)(2,1)}) custom-call(f32[1,4,2048]{2,1,0:T(4,128)} %state_ref.1, bf16[256,512]{1,0:T(8,128)(2,1)} %gate_hbm.1, bf16[256,512]{1,0:T(8,128)(2,1)} %up_hbm.1, bf16[512,256]{1,0:T(8,128)(2,1)} %down_hbm.1, ...), custom_call_target="tpu_custom_call" | custom-call | tf_op jit(solution)/shard_map/enter/pallas_call | solution.py:278
  3.2 9.1 %all-to-all-start = ((f32[16,16,128]{2,1,0:T(8,128)}), f32[16,16,128]{2,1,0:T(8,128)S(1)}, u32[]{:S(2)}, u32[]{:S(2)}) async-start(f32[16,16,128]{2,1,0:T(8,128)} %get-tuple-element.16), calls=%async_computation | async-start | bytes 262144 | tf_op jit(solution)/shard_map/all_to_all | solution.py:250
  12.3 2.7 %collective-permute-start = (bf16[3,256,256]{2,1,0:T(8,128)(2,1)}, bf16[3,256,256]{2,1,0:T(8,128)(2,1)}, u32[]{:S(2)}, u32[]{:S(2)}) collective-permute-start(bf16[3,256,256]{2,1,0:T(8,128)(2,1)} %get-tuple-element.21.refs_0_), channel_id=1, source_target_pairs={{16,0},{32,16},{48,32},{0,48},{17,1},{33,17},{49,33},{1,49},{18,2}... | collective-permute-start | bytes 1179656 | tf_op jit(solution)/shard_map/ppermute | solution.py:294
  15.0 0.3 collective-permute-start.1
  15.4 0.7 collective-permute-start.2
  16.1 0.7 collective-permute-start.3
  16.8 3.2 %all-to-all-done.rows_ref = f32[16,16,128]{2,1,0:T(8,128)S(1)} async-done(((f32[16,16,128]{2,1,0:T(8,128)}), f32[16,16,128]{2,1,0:T(8,128)S(1)}, u32[]{:S(2)}, u32[]{:S(2)}) %all-to-all-start) | async-done | bytes 131104 | tf_op jit(solution)/shard_map/all_to_all | solution.py:250
  20.0 0.7 copy-done.4
  20.6 9.3 %attend.1 = f32[16,16,128]{2,1,0:T(8,128)} custom-call(f32[16,16,128]{2,1,0:T(8,128)} %copy-done.4, s32[16]{0:T(128)} %length_ref.1, bf16[3,2048,128]{2,1,0:T(8,128)(2,1)} %weight_hbm.1, bf16[32832,128]{1,0:T(8,128)(2,1)} %bitcast.10, bf16[32832,128]{1,0:T(8,128)(2,1)} %bitcast.11, bf16[128,2048]{1,0:T(8,128)(2,1)} %out_weight_hbm.1), custom_call_target="tpu_custom_call" | custom-call | flops 3000000053248 | bytes 20971520 | tf_op jit(solution)/shard_map/attend/pallas_call | solution.py:305
  30.0 5.8 %all-to-all-start.1 = ((f32[16,16,128]{2,1,0:T(8,128)}), f32[16,16,128]{2,1,0:T(8,128)S(1)}, u32[]{:S(2)}, u32[]{:S(2)}) async-start(f32[16,16,128]{2,1,0:T(8,128)} %attend.1), calls=%async_computation.1 | async-start | bytes 262144 | tf_op jit(solution)/shard_map/all_to_all | solution.py:250
  35.8 2.1 %collective-permute-start.4 = (bf16[3,256,256]{2,1,0:T(8,128)(2,1)}, bf16[3,256,256]{2,1,0:T(8,128)(2,1)S(1)}, u32[]{:S(2)}, u32[]{:S(2)}) collective-permute-start(bf16[3,256,256]{2,1,0:T(8,128)(2,1)} %collective-permute-done.3.refs_4_), channel_id=1, source_target_pairs={{16,0},{32,16},{48,32},{0,48},{17,1},{33,17},{49,33},{1,49},{18,2}... | collective-permute-start | bytes 1179656 | tf_op jit(solution)/shard_map/ppermute | solution.py:294
  37.8 1.4 %collective-permute-start.5 = (bf16[3,256,256]{2,1,0:T(8,128)(2,1)}, bf16[3,256,256]{2,1,0:T(8,128)(2,1)S(1)}, u32[]{:S(2)}, u32[]{:S(2)}) collective-permute-start(bf16[3,256,256]{2,1,0:T(8,128)(2,1)} %collective-permute-done.3.refs_4_), channel_id=1, source_target_pairs={{32,0},{48,16},{0,32},{16,48},{33,1},{49,17},{1,33},{17,49},{34,2}... | collective-permute-start | bytes 1179656 | tf_op jit(solution)/shard_map/ppermute | solution.py:294
  39.3 0.0 collective-permute-start.6
  39.3 4.2 %all-to-all-done.1.received_ref = f32[16,16,128]{2,1,0:T(8,128)S(1)} async-done(((f32[16,16,128]{2,1,0:T(8,128)}), f32[16,16,128]{2,1,0:T(8,128)S(1)}, u32[]{:S(2)}, u32[]{:S(2)}) %all-to-all-start.1) | async-done | bytes 131104 | tf_op jit(solution)/shard_map/all_to_all | solution.py:250
  43.4 0.0 collective-permute-done.1.refs_2_
  43.4 0.0 collective-permute-done.2.refs_3_
  43.5 0.6 copy-done.3
  44.1 1.9 %middle.1 = (bf16[32,16,128]{2,1,0:T(8,128)(2,1)}, f32[4,16,128]{2,1,0:T(8,128)}) custom-call(f32[16,16,128]{2,1,0:T(8,128)} %copy-done.3, f32[4,16,128]{2,1,0:T(8,128)} %get-tuple-element.19.mixed_ref, f32[2,4]{1,0:T(2,128)} %width_ref.3, f32[2,4,4]{2,1,0:T(4,128)} %mix_ref.3, f32[2,4]{1,0:T(2,128)} %depth_ref.3), custom_call_target="tpu_custom_call" | custom-call | flops 2000000000 | bytes 1048576 | tf_op jit(solution)/shard_map/middle/pallas_call | solution.py:332
  45.9 12.2 %all_to_all.20.received_ref = bf16[32,16,128]{2,1,0:T(8,128)(2,1)} all-to-all(bf16[32,16,128]{2,1,0:T(8,128)(2,1)} %get-tuple-element.20), channel_id=1, replica_groups=mesh['zlo'=2,'y'=4,'blk'=16] {'zlo','blk'}, dimensions={0} | all-to-all | bytes 262144 | tf_op jit(solution)/shard_map/all_to_all | solution.py:250
  58.2 0.9 %collective-permute-done.6.refs_7_ = bf16[3,256,256]{2,1,0:T(8,128)(2,1)S(1)} collective-permute-done((bf16[3,256,256]{2,1,0:T(8,128)(2,1)}, bf16[3,256,256]{2,1,0:T(8,128)(2,1)S(1)}, u32[]{:S(2)}, u32[]{:S(2)}) %collective-permute-start.6) | collective-permute-done | bytes 393248 | tf_op jit(solution)/shard_map/ppermute | solution.py:294
  59.0 0.8 copy-done.2
  59.8 3.9 %feed.1 = bf16[32,16,128]{2,1,0:T(8,128)(2,1)} custom-call(bf16[32,16,128]{2,1,0:T(8,128)(2,1)} %all_to_all.20.received_ref, bf16[3,256,256]{2,1,0:T(8,128)(2,1)} %get-tuple-element.21.refs_0_, bf16[3,256,256]{2,1,0:T(8,128)(2,1)} %collective-permute-done.refs_1_, bf16[3,256,256]{2,1,0:T(8,128)(2,1)} %collective-permute-done.1.refs_2_, ...), custom_call_target="tpu_custom_call" | custom-call | tf_op jit(solution)/shard_map/feed/pallas_call | solution.py:345
  63.7 15.1 %all_to_all.21.received_ref = bf16[32,16,128]{2,1,0:T(8,128)(2,1)} all-to-all(bf16[32,16,128]{2,1,0:T(8,128)(2,1)} %feed.1), channel_id=1, replica_groups=mesh['zlo'=2,'y'=4,'blk'=16] {'zlo','blk'}, dimensions={0} | all-to-all | bytes 262144 | tf_op jit(solution)/shard_map/all_to_all | solution.py:250
  78.9 1.6 %leave.1 = f32[1,4,2048]{2,1,0:T(4,128)} custom-call(bf16[32,16,128]{2,1,0:T(8,128)(2,1)} %all_to_all.21.received_ref, f32[4,16,128]{2,1,0:T(8,128)} %get-tuple-element.26.base_ref, f32[2,4]{1,0:T(2,128)} %depth_ref.3), custom_call_target="tpu_custom_call" | custom-call | tf_op jit(solution)/shard_map/leave/pallas_call | solution.py:359
  (11 shorter events, 0.0 us)
Async XLA Ops:
  3.2 16.8 %all-to-all-start = ((f32[16,16,128]{2,1,0:T(8,128)}), f32[16,16,128]{2,1,0:T(8,128)S(1)}, u32[]{:S(2)}, u32[]{:S(2)}) async-start(f32[16,16,128]{2,1,0:T(8,128)} %get-tuple-element.16), calls=%async_computation | async-start | bytes 262144 | tf_op jit(solution)/shard_map/all_to_all | solution.py:250
  12.3 27.0 %collective-permute-start = (bf16[3,256,256]{2,1,0:T(8,128)(2,1)}, bf16[3,256,256]{2,1,0:T(8,128)(2,1)}, u32[]{:S(2)}, u32[]{:S(2)}) collective-permute-start(bf16[3,256,256]{2,1,0:T(8,128)(2,1)} %get-tuple-element.21.refs_0_), channel_id=1, source_target_pairs={{16,0},{32,16},{48,32},{0,48},{17,1},{33,17},{49,33},{1,49},{18,2}... | collective-permute-start | bytes 1179656 | tf_op jit(solution)/shard_map/ppermute | solution.py:294
  15.0 28.4 %collective-permute-start.1 = (bf16[3,256,256]{2,1,0:T(8,128)(2,1)}, bf16[3,256,256]{2,1,0:T(8,128)(2,1)}, u32[]{:S(2)}, u32[]{:S(2)}) collective-permute-start(bf16[3,256,256]{2,1,0:T(8,128)(2,1)} %get-tuple-element.21.refs_0_), channel_id=1, source_target_pairs={{32,0},{48,16},{0,32},{16,48},{33,1},{49,17},{1,33},{17,49},{34,2}... | collective-permute-start | bytes 1179656 | tf_op jit(solution)/shard_map/ppermute | solution.py:294
  15.4 28.1 %collective-permute-start.2 = (bf16[3,256,256]{2,1,0:T(8,128)(2,1)}, bf16[3,256,256]{2,1,0:T(8,128)(2,1)}, u32[]{:S(2)}, u32[]{:S(2)}) collective-permute-start(bf16[3,256,256]{2,1,0:T(8,128)(2,1)} %get-tuple-element.21.refs_0_), channel_id=1, source_target_pairs={{48,0},{0,16},{16,32},{32,48},{49,1},{1,17},{17,33},{33,49},{50,2}... | collective-permute-start | bytes 1179656 | tf_op jit(solution)/shard_map/ppermute | solution.py:294
  16.1 19.7 %collective-permute-start.3 = (bf16[3,256,256]{2,1,0:T(8,128)(2,1)}, bf16[3,256,256]{2,1,0:T(8,128)(2,1)}, u32[]{:S(2)}, u32[]{:S(2)}) collective-permute-start(bf16[3,256,256]{2,1,0:T(8,128)(2,1)} %get-tuple-element.25), channel_id=1, source_target_pairs={{0,64},{64,0},{1,65},{65,1},{2,66},{66,2},{3,67},{67,3},{4,68},{68... | collective-permute-start | bytes 1179656 | tf_op jit(solution)/shard_map/ppermute | solution.py:299
  20.0 0.7 copy-start.4
  30.0 13.5 %all-to-all-start.1 = ((f32[16,16,128]{2,1,0:T(8,128)}), f32[16,16,128]{2,1,0:T(8,128)S(1)}, u32[]{:S(2)}, u32[]{:S(2)}) async-start(f32[16,16,128]{2,1,0:T(8,128)} %attend.1), calls=%async_computation.1 | async-start | bytes 262144 | tf_op jit(solution)/shard_map/all_to_all | solution.py:250
  35.8 22.4 %collective-permute-start.4 = (bf16[3,256,256]{2,1,0:T(8,128)(2,1)}, bf16[3,256,256]{2,1,0:T(8,128)(2,1)S(1)}, u32[]{:S(2)}, u32[]{:S(2)}) collective-permute-start(bf16[3,256,256]{2,1,0:T(8,128)(2,1)} %collective-permute-done.3.refs_4_), channel_id=1, source_target_pairs={{16,0},{32,16},{48,32},{0,48},{17,1},{33,17},{49,33},{1,49},{18,2}... | collective-permute-start | bytes 1179656 | tf_op jit(solution)/shard_map/ppermute | solution.py:294
  37.8 20.3 %collective-permute-start.5 = (bf16[3,256,256]{2,1,0:T(8,128)(2,1)}, bf16[3,256,256]{2,1,0:T(8,128)(2,1)S(1)}, u32[]{:S(2)}, u32[]{:S(2)}) collective-permute-start(bf16[3,256,256]{2,1,0:T(8,128)(2,1)} %collective-permute-done.3.refs_4_), channel_id=1, source_target_pairs={{32,0},{48,16},{0,32},{16,48},{33,1},{49,17},{1,33},{17,49},{34,2}... | collective-permute-start | bytes 1179656 | tf_op jit(solution)/shard_map/ppermute | solution.py:294
  39.3 19.8 %collective-permute-start.6 = (bf16[3,256,256]{2,1,0:T(8,128)(2,1)}, bf16[3,256,256]{2,1,0:T(8,128)(2,1)S(1)}, u32[]{:S(2)}, u32[]{:S(2)}) collective-permute-start(bf16[3,256,256]{2,1,0:T(8,128)(2,1)} %collective-permute-done.3.refs_4_), channel_id=1, source_target_pairs={{48,0},{0,16},{16,32},{32,48},{49,1},{1,17},{17,33},{33,49},{50,2}... | collective-permute-start | bytes 1179656 | tf_op jit(solution)/shard_map/ppermute | solution.py:294
  43.4 0.6 copy-start.3
  58.1 0.9 %copy-start = (bf16[3,256,256]{2,1,0:T(8,128)(2,1)}, bf16[3,256,256]{2,1,0:T(8,128)(2,1)S(1)}, u32[]{:S(2)}) copy-start(bf16[3,256,256]{2,1,0:T(8,128)(2,1)S(1)} %collective-permute-done.4.refs_5_) | copy-start | bytes 1179652
  58.2 0.9 %copy-start.1 = (bf16[3,256,256]{2,1,0:T(8,128)(2,1)}, bf16[3,256,256]{2,1,0:T(8,128)(2,1)S(1)}, u32[]{:S(2)}) copy-start(bf16[3,256,256]{2,1,0:T(8,128)(2,1)S(1)} %collective-permute-done.5.refs_6_) | copy-start | bytes 1179652
  59.0 0.8 copy-start.2

commit v5 on v4

--- a/solution.py
+++ b/solution.py
@@ -286,6 +286,7 @@
         in_specs=[VMEM] + [HBM] * 3 + [SMEM] * 2,
         out_specs=[VMEM] * 4,
         scratch_shapes=[pltpu.VMEM((streams,) + tiles, f32), pltpu.SemaphoreType.DMA((6,))],
+        cost_estimate=pl.CostEstimate(flops=30 * 10**9, transcendentals=0, bytes_accessed=2**20),
         name="enter",
     )(hyper_state, w_gate, w_up, w_down, width_in, stream_mix)
 
@@ -315,7 +316,7 @@
             pltpu.VMEM((group, slots * group), f32),
             pltpu.SemaphoreType.DMA((2 + 2 * len(pieces),)),
         ],
-        compiler_params=pltpu.CompilerParams(vmem_limit_bytes=63 * 2**20),
+        compiler_params=pltpu.CompilerParams(vmem_limit_bytes=50 * 2**20),
         cost_estimate=pl.CostEstimate(flops=3 * 10**12, transcendentals=0, bytes_accessed=20 * 2**20),
         name="attend",
     )(
@@ -338,6 +339,7 @@
         in_specs=[VMEM] * 2 + [SMEM] * 3,
         out_specs=[VMEM] * 2,
         cost_estimate=pl.CostEstimate(flops=2 * 10**9, transcendentals=0, bytes_accessed=2**20),
+        compiler_params=pltpu.CompilerParams(vmem_limit_bytes=16 * 2**20),
         name="middle",
     )(received, mixed, width_in, stream_mix, depth_out)
     received = exchange(send, plane)
@@ -352,6 +354,7 @@
             pltpu.VMEM((plane_count,) + tiles, f32),
             pltpu.SemaphoreType.DMA((2 * ring,)),
         ],
+        compiler_params=pltpu.CompilerParams(vmem_limit_bytes=16 * 2**20),
         name="feed",
     )(received, *near, *far)
     received = exchange(send, plane)

time: 81 us -> 77 us (0.951)
  Pallas kernels: 19.8 us -> 16.6 us
  waiting for transfers between devices: 8.22 us -> 10.9 us
  local copies, waits for them, and re-layouts: 2.07 us -> 0.04 us
  blocking collectives: 27.3 us -> 26 us
    ppermute x6, waiting for transfers between devices: 0.88 us -> 3.53 us  [gathered(): lax.ppermute(array, 'y', [((place + distance) % ring, place) for place in...]
    unnamed x10 -> x18, local copies, waits for them, and re-layouts: 2.07 us -> 0.04 us
    pallas_call x1, Pallas kernels: 3.92 us -> 2.27 us  [on_device(): pl.pallas_call(feed_kernel, out_shape=jax.ShapeDtypeStruct((plane_count,)...]
    all_to_all x2, blocking collectives: 27.3 us -> 26 us  [exchange(): return lax.all_to_all(rows, axes, split_axis=0, concat_axis=0, tiled=True)]
    pallas_call x1, Pallas kernels: 1.85 us -> 0.9 us  [on_device(): pl.pallas_call(middle_kernel, out_shape=[jax.ShapeDtypeStruct((plane_coun...]
  transfers between devices with their start and end apart: 9 -> 9, of which waited for: 3 -> 3; matrix products, arithmetic and copies ran while one was open for 0% -> 0% of each run, Pallas kernels for 14% -> 12%
where the time goes in v5:
time: 77 us; the launch traced here: 76.6 us
  blocking collectives  26 us (34%)
  starting transfers between devices  23 us (30%)
  Pallas kernels  16.6 us (22%)
  waiting for transfers between devices  10.9 us (14%)
    all_to_all x2, blocking collectives, exchange(): return lax.all_to_all(rows, axes, split_axis=0, concat_axis=0, tiled=True)  26 us
    all_to_all x2, starting transfers between devices, exchange(): return lax.all_to_all(rows, axes, split_axis=0, concat_axis=0, tiled=True)  15 us
    pallas_call x1, Pallas kernels, on_device(): pl.pallas_call(functools.partial(attend_kernel, pieces=pieces, steps=step...  8.61 us
    all_to_all x2, waiting for transfers between devices, exchange(): return lax.all_to_all(rows, axes, split_axis=0, concat_axis=0, tiled=True)  7.34 us
    ppermute x6, starting transfers between devices, gathered(): lax.ppermute(array, 'y', [((place + distance) % ring, place) for place in...  7.27 us
    ppermute x6, waiting for transfers between devices, gathered(): lax.ppermute(array, 'y', [((place + distance) % ring, place) for place in...  3.53 us
    pallas_call x1, Pallas kernels, on_device(): pl.pallas_call(enter_kernel, out_shape=[jax.ShapeDtypeStruct((blk_count,)...  3.21 us
    pallas_call x1, Pallas kernels, on_device(): pl.pallas_call(feed_kernel, out_shape=jax.ShapeDtypeStruct((plane_count,)...  2.27 us
  transfers between devices with their start and end apart: 9, of which 3 were waited for; matrix products, arithmetic and copies ran while one was open for 0% of the time, Pallas kernels for 12%

profile of v5, /device:TPU:1, one launch (start us, length us, event | category | flops | bytes accessed | tf_op | source)
XLA Modules:
  0.0 76.6 jit_solution(744929682517524459)
XLA Ops:
  0.0 3.2 %enter.1 = (f32[16,16,128]{2,1,0:T(8,128)}, f32[4,16,128]{2,1,0:T(8,128)}, bf16[3,256,256]{2,1,0:T(8,128)(2,1)}, bf16[3,256,256]{2,1,0:T(8,128)(2,1)}) custom-call(f32[1,4,2048]{2,1,0:T(4,128)} %state_ref.1, bf16[256,512]{1,0:T(8,128)(2,1)} %gate_hbm.1, bf16[256,512]{1,0:T(8,128)(2,1)} %up_hbm.1, bf16[512,256]{1,0:T(8,128)(2,1)} %down_hbm.1, ...), custom_call_target="tpu_custom_call" | custom-call | flops 30000001024 | bytes 1048576 | tf_op jit(solution)/shard_map/enter/pallas_call | solution.py:278
  3.2 9.1 %all-to-all-start = ((f32[16,16,128]{2,1,0:T(8,128)}), f32[16,16,128]{2,1,0:T(8,128)S(1)}, u32[]{:S(2)}, u32[]{:S(2)}) async-start(f32[16,16,128]{2,1,0:T(8,128)} %get-tuple-element.16), calls=%async_computation | async-start | bytes 262144 | tf_op jit(solution)/shard_map/all_to_all | solution.py:250
  12.4 2.7 %collective-permute-start = (bf16[3,256,256]{2,1,0:T(8,128)(2,1)}, bf16[3,256,256]{2,1,0:T(8,128)(2,1)}, u32[]{:S(2)}, u32[]{:S(2)}) collective-permute-start(bf16[3,256,256]{2,1,0:T(8,128)(2,1)} %get-tuple-element.21.refs_0_), channel_id=1, source_target_pairs={{16,0},{32,16},{48,32},{0,48},{17,1},{33,17},{49,33},{1,49},{18,2}... | collective-permute-start | bytes 1179656 | tf_op jit(solution)/shard_map/ppermute | solution.py:295
  15.1 0.3 collective-permute-start.1
  15.5 0.7 collective-permute-start.2
  16.1 0.7 collective-permute-start.3
  16.9 3.2 %all-to-all-done.rows_ref = f32[16,16,128]{2,1,0:T(8,128)S(1)} async-done(((f32[16,16,128]{2,1,0:T(8,128)}), f32[16,16,128]{2,1,0:T(8,128)S(1)}, u32[]{:S(2)}, u32[]{:S(2)}) %all-to-all-start) | async-done | bytes 131104 | tf_op jit(solution)/shard_map/all_to_all | solution.py:250
  20.1 0.0 copy-start.2
  20.1 0.0 copy-start.5
  20.1 0.0 copy-start.6
  20.1 0.0 copy-start.8
  20.1 8.6 %attend.1 = f32[16,16,128]{2,1,0:T(8,128)} custom-call(f32[16,16,128]{2,1,0:T(8,128)S(1)} %all-to-all-done.rows_ref, s32[16]{0:T(128)S(1)} %copy-done.7, bf16[3,2048,128]{2,1,0:T(8,128)(2,1)S(1)} %copy-done.3, bf16[32832,128]{1,0:T(8,128)(2,1)} %bitcast.10, bf16[32832,128]{1,0:T(8,128)(2,1)} %bitcast.11, bf16[128,2048]{1,0:T(8,128)(2,1)S(1)} %copy-done.4), custom_call_target="tpu_custom_call" | custom-call | flops 3000000053248 | bytes 20971520 | tf_op jit(solution)/shard_map/attend/pallas_call | solution.py:306
  28.7 5.8 %all-to-all-start.1 = ((f32[16,16,128]{2,1,0:T(8,128)}), f32[16,16,128]{2,1,0:T(8,128)S(1)}, u32[]{:S(2)}, u32[]{:S(2)}) async-start(f32[16,16,128]{2,1,0:T(8,128)} %attend.1), calls=%async_computation.1 | async-start | bytes 262144 | tf_op jit(solution)/shard_map/all_to_all | solution.py:250
  34.5 2.1 %collective-permute-start.4 = (bf16[3,256,256]{2,1,0:T(8,128)(2,1)}, bf16[3,256,256]{2,1,0:T(8,128)(2,1)S(1)}, u32[]{:S(2)}, u32[]{:S(2)}) collective-permute-start(bf16[3,256,256]{2,1,0:T(8,128)(2,1)} %collective-permute-done.3.refs_4_), channel_id=1, source_target_pairs={{16,0},{32,16},{48,32},{0,48},{17,1},{33,17},{49,33},{1,49},{18,2}... | collective-permute-start | bytes 1179656 | tf_op jit(solution)/shard_map/ppermute | solution.py:295
  36.6 1.4 %collective-permute-start.5 = (bf16[3,256,256]{2,1,0:T(8,128)(2,1)}, bf16[3,256,256]{2,1,0:T(8,128)(2,1)S(1)}, u32[]{:S(2)}, u32[]{:S(2)}) collective-permute-start(bf16[3,256,256]{2,1,0:T(8,128)(2,1)} %collective-permute-done.3.refs_4_), channel_id=1, source_target_pairs={{32,0},{48,16},{0,32},{16,48},{33,1},{49,17},{1,33},{17,49},{34,2}... | collective-permute-start | bytes 1179656 | tf_op jit(solution)/shard_map/ppermute | solution.py:295
  38.0 4.2 %all-to-all-done.1.received_ref = f32[16,16,128]{2,1,0:T(8,128)S(1)} async-done(((f32[16,16,128]{2,1,0:T(8,128)}), f32[16,16,128]{2,1,0:T(8,128)S(1)}, u32[]{:S(2)}, u32[]{:S(2)}) %all-to-all-start.1) | async-done | bytes 131104 | tf_op jit(solution)/shard_map/all_to_all | solution.py:250
  42.2 0.0 collective-permute-done.1.refs_2_
  42.3 0.9 %middle.1 = (bf16[32,16,128]{2,1,0:T(8,128)(2,1)S(1)}, f32[4,16,128]{2,1,0:T(8,128)S(1)}) custom-call(f32[16,16,128]{2,1,0:T(8,128)S(1)} %all-to-all-done.1.received_ref, f32[4,16,128]{2,1,0:T(8,128)S(1)} %copy-done.8, f32[2,4]{1,0:T(2,128)S(1)} %copy-done.6, f32[2,4,4]{2,1,0:T(4,128)S(1)} %copy-done.5, f32[2,4]{1,0:T(2,128)S(1)} %copy-done.2), custom_call_target="tpu_custom_call" | custom-call | flops 2000000000 | bytes 1048576 | tf_op jit(solution)/shard_map/middle/pallas_call | solution.py:333
  43.2 11.1 %all_to_all.20.received_ref = bf16[32,16,128]{2,1,0:T(8,128)(2,1)S(1)} all-to-all(bf16[32,16,128]{2,1,0:T(8,128)(2,1)S(1)} %get-tuple-element.20), channel_id=1, replica_groups=mesh['zlo'=2,'y'=4,'blk'=16] {'zlo','blk'}, dimensions={0} | all-to-all | bytes 262144 | tf_op jit(solution)/shard_map/all_to_all | solution.py:250
  54.3 0.0 collective-permute-done.4.refs_5_
  54.3 3.5 %collective-permute-done.6.refs_7_ = bf16[3,256,256]{2,1,0:T(8,128)(2,1)S(1)} collective-permute-done((bf16[3,256,256]{2,1,0:T(8,128)(2,1)}, bf16[3,256,256]{2,1,0:T(8,128)(2,1)S(1)}, u32[]{:S(2)}, u32[]{:S(2)}) %collective-permute-start.6) | collective-permute-done | bytes 393248 | tf_op jit(solution)/shard_map/ppermute | solution.py:295
  57.8 2.3 %feed.1 = bf16[32,16,128]{2,1,0:T(8,128)(2,1)S(1)} custom-call(bf16[32,16,128]{2,1,0:T(8,128)(2,1)S(1)} %all_to_all.20.received_ref, bf16[3,256,256]{2,1,0:T(8,128)(2,1)S(1)} %copy-done, bf16[3,256,256]{2,1,0:T(8,128)(2,1)} %collective-permute-done.refs_1_, bf16[3,256,256]{2,1,0:T(8,128)(2,1)} %collective-permute-done.1.refs_2_, ...), custom_call_target="tpu_custom_call" | custom-call | tf_op jit(solution)/shard_map/feed/pallas_call | solution.py:347
  60.1 14.9 %all_to_all.21.received_ref = bf16[32,16,128]{2,1,0:T(8,128)(2,1)} all-to-all(bf16[32,16,128]{2,1,0:T(8,128)(2,1)S(1)} %feed.1), channel_id=1, replica_groups=mesh['zlo'=2,'y'=4,'blk'=16] {'zlo','blk'}, dimensions={0} | all-to-all | bytes 262144 | tf_op jit(solution)/shard_map/all_to_all | solution.py:250
  75.0 1.6 %leave.1 = f32[1,4,2048]{2,1,0:T(4,128)} custom-call(bf16[32,16,128]{2,1,0:T(8,128)(2,1)} %all_to_all.21.received_ref, f32[4,16,128]{2,1,0:T(8,128)} %copy-done.1, f32[2,4]{1,0:T(2,128)} %depth_ref.3), custom_call_target="tpu_custom_call" | custom-call | tf_op jit(solution)/shard_map/leave/pallas_call | solution.py:362
  (19 shorter events, 0.0 us)
Async XLA Ops:
  0.0 20.0 %copy-start.7 = (s32[16]{0:T(128)S(1)}, s32[16]{0:T(128)}, u32[]{:S(2)}) copy-start(s32[16]{0:T(128)} %length_ref.1) | copy-start | bytes 196
  0.0 20.0 %copy-start.3 = (bf16[3,2048,128]{2,1,0:T(8,128)(2,1)S(1)}, bf16[3,2048,128]{2,1,0:T(8,128)(2,1)}, u32[]{:S(2)}) copy-start(bf16[3,2048,128]{2,1,0:T(8,128)(2,1)} %weight_hbm.1) | copy-start | bytes 4718596
  0.0 20.0 %copy-start.4 = (bf16[128,2048]{1,0:T(8,128)(2,1)S(1)}, bf16[128,2048]{1,0:T(8,128)(2,1)}, u32[]{:S(2)}) copy-start(bf16[128,2048]{1,0:T(8,128)(2,1)} %out_weight_hbm.1) | copy-start | bytes 1572868
  3.2 16.8 %all-to-all-start = ((f32[16,16,128]{2,1,0:T(8,128)}), f32[16,16,128]{2,1,0:T(8,128)S(1)}, u32[]{:S(2)}, u32[]{:S(2)}) async-start(f32[16,16,128]{2,1,0:T(8,128)} %get-tuple-element.16), calls=%async_computation | async-start | bytes 262144 | tf_op jit(solution)/shard_map/all_to_all | solution.py:250
  12.4 25.7 %collective-permute-start = (bf16[3,256,256]{2,1,0:T(8,128)(2,1)}, bf16[3,256,256]{2,1,0:T(8,128)(2,1)}, u32[]{:S(2)}, u32[]{:S(2)}) collective-permute-start(bf16[3,256,256]{2,1,0:T(8,128)(2,1)} %get-tuple-element.21.refs_0_), channel_id=1, source_target_pairs={{16,0},{32,16},{48,32},{0,48},{17,1},{33,17},{49,33},{1,49},{18,2}... | collective-permute-start | bytes 1179656 | tf_op jit(solution)/shard_map/ppermute | solution.py:295
  15.1 27.1 %collective-permute-start.1 = (bf16[3,256,256]{2,1,0:T(8,128)(2,1)}, bf16[3,256,256]{2,1,0:T(8,128)(2,1)}, u32[]{:S(2)}, u32[]{:S(2)}) collective-permute-start(bf16[3,256,256]{2,1,0:T(8,128)(2,1)} %get-tuple-element.21.refs_0_), channel_id=1, source_target_pairs={{32,0},{48,16},{0,32},{16,48},{33,1},{49,17},{1,33},{17,49},{34,2}... | collective-permute-start | bytes 1179656 | tf_op jit(solution)/shard_map/ppermute | solution.py:295
  15.5 26.8 %collective-permute-start.2 = (bf16[3,256,256]{2,1,0:T(8,128)(2,1)}, bf16[3,256,256]{2,1,0:T(8,128)(2,1)}, u32[]{:S(2)}, u32[]{:S(2)}) collective-permute-start(bf16[3,256,256]{2,1,0:T(8,128)(2,1)} %get-tuple-element.21.refs_0_), channel_id=1, source_target_pairs={{48,0},{0,16},{16,32},{32,48},{49,1},{1,17},{17,33},{33,49},{50,2}... | collective-permute-start | bytes 1179656 | tf_op jit(solution)/shard_map/ppermute | solution.py:295
  16.1 18.4 %collective-permute-start.3 = (bf16[3,256,256]{2,1,0:T(8,128)(2,1)}, bf16[3,256,256]{2,1,0:T(8,128)(2,1)}, u32[]{:S(2)}, u32[]{:S(2)}) collective-permute-start(bf16[3,256,256]{2,1,0:T(8,128)(2,1)} %get-tuple-element.25), channel_id=1, source_target_pairs={{0,64},{64,0},{1,65},{65,1},{2,66},{66,2},{3,67},{67,3},{4,68},{68... | collective-permute-start | bytes 1179656 | tf_op jit(solution)/shard_map/ppermute | solution.py:300
  20.1 22.2 %copy-start.2 = (f32[2,4]{1,0:T(2,128)S(1)}, f32[2,4]{1,0:T(2,128)}, u32[]{:S(2)}) copy-start(f32[2,4]{1,0:T(2,128)} %depth_ref.3) | copy-start | bytes 100
  20.1 22.2 %copy-start.5 = (f32[2,4,4]{2,1,0:T(4,128)S(1)}, f32[2,4,4]{2,1,0:T(4,128)}, u32[]{:S(2)}) copy-start(f32[2,4,4]{2,1,0:T(4,128)} %mix_ref.3) | copy-start | bytes 388
  20.1 22.2 %copy-start.6 = (f32[2,4]{1,0:T(2,128)S(1)}, f32[2,4]{1,0:T(2,128)}, u32[]{:S(2)}) copy-start(f32[2,4]{1,0:T(2,128)} %width_ref.3) | copy-start | bytes 100
  20.1 22.2 %copy-start.8 = (f32[4,16,128]{2,1,0:T(8,128)S(1)}, f32[4,16,128]{2,1,0:T(8,128)}, u32[]{:S(2)}) copy-start(f32[4,16,128]{2,1,0:T(8,128)} %get-tuple-element.19.mixed_ref) | copy-start | bytes 98308
  20.1 37.7 %copy-start = (bf16[3,256,256]{2,1,0:T(8,128)(2,1)S(1)}, bf16[3,256,256]{2,1,0:T(8,128)(2,1)}, u32[]{:S(2)}) copy-start(bf16[3,256,256]{2,1,0:T(8,128)(2,1)} %get-tuple-element.21.refs_0_) | copy-start | bytes 1179652
  28.7 13.5 %all-to-all-start.1 = ((f32[16,16,128]{2,1,0:T(8,128)}), f32[16,16,128]{2,1,0:T(8,128)S(1)}, u32[]{:S(2)}, u32[]{:S(2)}) async-start(f32[16,16,128]{2,1,0:T(8,128)} %attend.1), calls=%async_computation.1 | async-start | bytes 262144 | tf_op jit(solution)/shard_map/all_to_all | solution.py:250
  34.5 19.7 %collective-permute-start.4 = (bf16[3,256,256]{2,1,0:T(8,128)(2,1)}, bf16[3,256,256]{2,1,0:T(8,128)(2,1)S(1)}, u32[]{:S(2)}, u32[]{:S(2)}) collective-permute-start(bf16[3,256,256]{2,1,0:T(8,128)(2,1)} %collective-permute-done.3.refs_4_), channel_id=1, source_target_pairs={{16,0},{32,16},{48,32},{0,48},{17,1},{33,17},{49,33},{1,49},{18,2}... | collective-permute-start | bytes 1179656 | tf_op jit(solution)/shard_map/ppermute | solution.py:295
  36.6 17.7 %collective-permute-start.5 = (bf16[3,256,256]{2,1,0:T(8,128)(2,1)}, bf16[3,256,256]{2,1,0:T(8,128)(2,1)S(1)}, u32[]{:S(2)}, u32[]{:S(2)}) collective-permute-start(bf16[3,256,256]{2,1,0:T(8,128)(2,1)} %collective-permute-done.3.refs_4_), channel_id=1, source_target_pairs={{32,0},{48,16},{0,32},{16,48},{33,1},{49,17},{1,33},{17,49},{34,2}... | collective-permute-start | bytes 1179656 | tf_op jit(solution)/shard_map/ppermute | solution.py:295
  38.0 19.8 %collective-permute-start.6 = (bf16[3,256,256]{2,1,0:T(8,128)(2,1)}, bf16[3,256,256]{2,1,0:T(8,128)(2,1)S(1)}, u32[]{:S(2)}, u32[]{:S(2)}) collective-permute-start(bf16[3,256,256]{2,1,0:T(8,128)(2,1)} %collective-permute-done.3.refs_4_), channel_id=1, source_target_pairs={{48,0},{0,16},{16,32},{32,48},{49,1},{1,17},{17,33},{33,49},{50,2}... | collective-permute-start | bytes 1179656 | tf_op jit(solution)/shard_map/ppermute | solution.py:295
  43.2 31.8 %copy-start.1 = (f32[4,16,128]{2,1,0:T(8,128)}, f32[4,16,128]{2,1,0:T(8,128)S(1)}, u32[]{:S(2)}) copy-start(f32[4,16,128]{2,1,0:T(8,128)S(1)} %get-tuple-element.26.base_ref) | copy-start | bytes 98308

commit v6 on v5

--- a/solution.py
+++ b/solution.py
@@ -54,7 +54,8 @@
         tiles[:, row, :] = state_ref[0, :, row * LANES : (row + 1) * LANES]
     state = [tiles[stream] for stream in range(streams)]
     combined = sum(width_ref[0, stream] * state[stream] for stream in range(streams))
-    send_ref[...] = jnp.broadcast_to(normalize(combined)[None], send_ref.shape)
+    normed = normalize(combined).astype(send_ref.dtype)
+    send_ref[...] = jnp.broadcast_to(normed[None], send_ref.shape)
     for target in range(streams):
         mixed_ref[target] = sum(mix_ref[0, stream, target] * state[stream] for stream in range(streams))
     for copy in copies:
@@ -84,6 +85,7 @@
     keys,
     values,
     scores,
+    tiles,
     sems,
     *,
     pieces,
@@ -118,7 +120,8 @@
     for row in range(group):
         lengths = jnp.where(request == row, length_ref[row], lengths)
     cosine, sine = turn_tables(lengths)
-    rows = jnp.concatenate([rows_ref[:, row, :] for row in range(rows_ref.shape[1])], axis=1)
+    tiles[...] = rows_ref[...].astype(jnp.float32)
+    rows = jnp.concatenate([tiles[:, row, :] for row in range(tiles.shape[1])], axis=1)
     rows = rows.astype(jnp.bfloat16)
     arrive()
     projected = [
@@ -174,13 +177,14 @@
     attended = (mixed / denom).astype(jnp.bfloat16)
     arrive()
     part = jnp.dot(attended, out_weight_ref[...], preferred_element_type=jnp.float32)
-    for row in range(send_ref.shape[1]):
-        send_ref[:, row, :] = part[:, row * LANES : (row + 1) * LANES]
+    for row in range(tiles.shape[1]):
+        tiles[:, row, :] = part[:, row * LANES : (row + 1) * LANES]
+    send_ref[...] = tiles[...].astype(send_ref.dtype)
 
 
 def middle_kernel(received_ref, mixed_ref, width_ref, mix_ref, depth_ref, send_ref, base_ref):
     streams = mixed_ref.shape[0]
-    attn_out = jnp.sum(received_ref[...], axis=0)
+    attn_out = jnp.sum(received_ref[...].astype(jnp.float32), axis=0)
     state = [mixed_ref[stream] + depth_ref[0, stream] * attn_out for stream in range(streams)]
     combined = sum(width_ref[1, stream] * state[stream] for stream in range(streams))
     normed = normalize(combined)
@@ -278,7 +282,7 @@
     send, mixed, own, sent = pl.pallas_call(
         enter_kernel,
         out_shape=[
-            jax.ShapeDtypeStruct((blk_count,) + tiles, f32),
+            jax.ShapeDtypeStruct((blk_count,) + tiles, bf16),
             jax.ShapeDtypeStruct((streams,) + tiles, f32),
             piece,
             piece,
@@ -305,7 +309,7 @@
     steps = cut(slots * group, 8192)
     send = pl.pallas_call(
         functools.partial(attend_kernel, pieces=pieces, steps=steps),
-        out_shape=jax.ShapeDtypeStruct((group,) + tiles, f32),
+        out_shape=jax.ShapeDtypeStruct((group,) + tiles, bf16),
         in_specs=[VMEM, SMEM] + [HBM] * 4,
         out_specs=VMEM,
         scratch_shapes=[
@@ -314,6 +318,7 @@
             pltpu.VMEM((slots * group, head), bf16),
             pltpu.VMEM((slots * group, head), bf16),
             pltpu.VMEM((group, slots * group), f32),
+            pltpu.VMEM((group,) + tiles, f32),
             pltpu.SemaphoreType.DMA((2 + 2 * len(pieces),)),
         ],
         compiler_params=pltpu.CompilerParams(vmem_limit_bytes=50 * 2**20),

time: 77 us -> 74.6 us (0.969)
  blocking collectives: 26 us -> 36.7 us
  waiting for transfers between devices: 10.9 us -> 2.94 us
  starting transfers between devices: 23 us -> 18.3 us
    all_to_all x2 -> x3, blocking collectives: 26 us -> 36.7 us  [exchange(): return lax.all_to_all(rows, axes, split_axis=0, concat_axis=0, tiled=True)]
    all_to_all x2 -> x1, starting transfers between devices: 15 us -> 8.57 us  [exchange(): return lax.all_to_all(rows, axes, split_axis=0, concat_axis=0, tiled=True)]
    all_to_all x2 -> x1, waiting for transfers between devices: 7.34 us -> 2.92 us  [exchange(): return lax.all_to_all(rows, axes, split_axis=0, concat_axis=0, tiled=True)]
    ppermute x6, waiting for transfers between devices: 3.53 us -> 0.02 us  [gathered(): lax.ppermute(array, 'y', [((place + distance) % ring, place) for place in...]
    ppermute x1, starting transfers between devices: 0.74 us -> 2.55 us  [on_device(): far = gathered(lax.ppermute(sent, 'zlo', [(0, 1), (1, 0)]))]
  transfers between devices with their start and end apart: 9 -> 8, of which waited for: 3 -> 1; matrix products, arithmetic and copies ran while one was open for 0% -> 0% of each run, Pallas kernels for 12% -> 12%
where the time goes in v6:
time: 74.6 us; the launch traced here: 74.2 us
  blocking collectives  36.7 us (49%)
  starting transfers between devices  18.3 us (25%)
  Pallas kernels  16.1 us (22%)
  waiting for transfers between devices  2.94 us (4%)
    all_to_all x3, blocking collectives, exchange(): return lax.all_to_all(rows, axes, split_axis=0, concat_axis=0, tiled=True)  36.7 us
    all_to_all x1, starting transfers between devices, exchange(): return lax.all_to_all(rows, axes, split_axis=0, concat_axis=0, tiled=True)  8.57 us
    pallas_call x1, Pallas kernels, on_device(): pl.pallas_call(functools.partial(attend_kernel, pieces=pieces, steps=step...  7.97 us
    ppermute x6, starting transfers between devices, gathered(): lax.ppermute(array, 'y', [((place + distance) % ring, place) for place in...  7.17 us
    pallas_call x1, Pallas kernels, on_device(): pl.pallas_call(enter_kernel, out_shape=[jax.ShapeDtypeStruct((blk_count,)...  3.16 us
    all_to_all x1, waiting for transfers between devices, exchange(): return lax.all_to_all(rows, axes, split_axis=0, concat_axis=0, tiled=True)  2.92 us
    ppermute x1, starting transfers between devices, on_device(): far = gathered(lax.ppermute(sent, 'zlo', [(0, 1), (1, 0)]))  2.55 us
    pallas_call x1, Pallas kernels, on_device(): pl.pallas_call(feed_kernel, out_shape=jax.ShapeDtypeStruct((plane_count,)...  2.52 us
  transfers between devices with their start and end apart: 8, of which 1 were waited for; matrix products, arithmetic and copies ran while one was open for 0% of the time, Pallas kernels for 12%

profile of v6, /device:TPU:1, one launch (start us, length us, event | category | flops | bytes accessed | tf_op | source)
XLA Modules:
  0.0 74.2 jit_solution(17932215557919847991)
XLA Ops:
  0.0 3.2 %enter.1 = (bf16[16,16,128]{2,1,0:T(8,128)(2,1)}, f32[4,16,128]{2,1,0:T(8,128)}, bf16[3,256,256]{2,1,0:T(8,128)(2,1)}, bf16[3,256,256]{2,1,0:T(8,128)(2,1)}) custom-call(f32[1,4,2048]{2,1,0:T(4,128)} %state_ref.1, bf16[256,512]{1,0:T(8,128)(2,1)} %gate_hbm.1, bf16[256,512]{1,0:T(8,128)(2,1)} %up_hbm.1, bf16[512,256]{1,0:T(8,128)(2,1)} %down_hbm.1, ...), custom_call_target="tpu_custom_call" | custom-call | flops 30000001024 | bytes 1048576 | tf_op jit(solution)/shard_map/enter/pallas_call | solution.py:282
  3.2 2.5 %collective-permute-start.3 = (bf16[3,256,256]{2,1,0:T(8,128)(2,1)}, bf16[3,256,256]{2,1,0:T(8,128)(2,1)}, u32[]{:S(2)}, u32[]{:S(2)}) collective-permute-start(bf16[3,256,256]{2,1,0:T(8,128)(2,1)} %get-tuple-element.25), channel_id=1, source_target_pairs={{0,64},{64,0},{1,65},{65,1},{2,66},{66,2},{3,67},{67,3},{4,68},{68... | collective-permute-start | bytes 1179656 | tf_op jit(solution)/shard_map/ppermute | solution.py:304
  5.7 2.7 %collective-permute-start = (bf16[3,256,256]{2,1,0:T(8,128)(2,1)}, bf16[3,256,256]{2,1,0:T(8,128)(2,1)S(1)}, u32[]{:S(2)}, u32[]{:S(2)}) collective-permute-start(bf16[3,256,256]{2,1,0:T(8,128)(2,1)} %get-tuple-element.21.refs_0_), channel_id=1, source_target_pairs={{16,0},{32,16},{48,32},{0,48},{17,1},{33,17},{49,33},{1,49},{18,2}... | collective-permute-start | bytes 1179656 | tf_op jit(solution)/shard_map/ppermute | solution.py:299
  8.5 8.6 %all-to-all-start = ((bf16[16,16,128]{2,1,0:T(8,128)(2,1)}), bf16[16,16,128]{2,1,0:T(8,128)(2,1)S(1)}, u32[]{:S(2)}, u32[]{:S(2)}) async-start(bf16[16,16,128]{2,1,0:T(8,128)(2,1)} %get-tuple-element.16), calls=%async_computation | async-start | bytes 131072 | tf_op jit(solution)/shard_map/all_to_all | solution.py:254
  17.0 0.3 collective-permute-start.1
  17.4 0.7 collective-permute-start.2
  18.1 0.0 collective-permute-done.3.refs_4_
  18.1 2.0 %collective-permute-start.4 = (bf16[3,256,256]{2,1,0:T(8,128)(2,1)}, bf16[3,256,256]{2,1,0:T(8,128)(2,1)}, u32[]{:S(2)}, u32[]{:S(2)}) collective-permute-start(bf16[3,256,256]{2,1,0:T(8,128)(2,1)} %collective-permute-done.3.refs_4_), channel_id=1, source_target_pairs={{16,0},{32,16},{48,32},{0,48},{17,1},{33,17},{49,33},{1,49},{18,2}... | collective-permute-start | bytes 1179656 | tf_op jit(solution)/shard_map/ppermute | solution.py:299
  20.1 1.4 %collective-permute-start.5 = (bf16[3,256,256]{2,1,0:T(8,128)(2,1)}, bf16[3,256,256]{2,1,0:T(8,128)(2,1)}, u32[]{:S(2)}, u32[]{:S(2)}) collective-permute-start(bf16[3,256,256]{2,1,0:T(8,128)(2,1)} %collective-permute-done.3.refs_4_), channel_id=1, source_target_pairs={{32,0},{48,16},{0,32},{16,48},{33,1},{49,17},{1,33},{17,49},{34,2}... | collective-permute-start | bytes 1179656 | tf_op jit(solution)/shard_map/ppermute | solution.py:299
  21.5 0.0 collective-permute-done.refs_1_
  21.5 0.0 collective-permute-start.6
  21.5 2.9 %all-to-all-done.rows_ref = bf16[16,16,128]{2,1,0:T(8,128)(2,1)S(1)} async-done(((bf16[16,16,128]{2,1,0:T(8,128)(2,1)}), bf16[16,16,128]{2,1,0:T(8,128)(2,1)S(1)}, u32[]{:S(2)}, u32[]{:S(2)}) %all-to-all-start) | async-done | bytes 65568 | tf_op jit(solution)/shard_map/all_to_all | solution.py:254
  24.4 0.0 copy-start.2
  24.4 0.0 copy-start.5
  24.4 0.0 copy-start.6
  24.4 0.0 copy-start.8
  24.5 8.0 %attend.1 = bf16[16,16,128]{2,1,0:T(8,128)(2,1)S(1)} custom-call(bf16[16,16,128]{2,1,0:T(8,128)(2,1)S(1)} %all-to-all-done.rows_ref, s32[16]{0:T(128)S(1)} %copy-done.7, bf16[3,2048,128]{2,1,0:T(8,128)(2,1)S(1)} %copy-done.3, bf16[32832,128]{1,0:T(8,128)(2,1)} %bitcast.10, bf16[32832,128]{1,0:T(8,128)(2,1)} %bitcast.11, bf16[128,2048]{1,0:T(8,128)(2,1)S(1)} %copy-done.4), custom_call_target="tpu_custom_call" | custom-call | flops 3000000053248 | bytes 20971520 | tf_op jit(solution)/shard_map/attend/pallas_call | solution.py:310
  32.4 12.6 %all_to_all.20.received_ref = bf16[16,16,128]{2,1,0:T(8,128)(2,1)S(1)} all-to-all(bf16[16,16,128]{2,1,0:T(8,128)(2,1)S(1)} %attend.1), channel_id=1, replica_groups=mesh['zlo'=2,'y'=4,'blk'=16] {'blk'}, dimensions={0} | all-to-all | bytes 131072 | tf_op jit(solution)/shard_map/all_to_all | solution.py:254
  45.1 0.9 %middle.1 = (bf16[32,16,128]{2,1,0:T(8,128)(2,1)S(1)}, f32[4,16,128]{2,1,0:T(8,128)S(1)}) custom-call(bf16[16,16,128]{2,1,0:T(8,128)(2,1)S(1)} %all_to_all.20.received_ref, f32[4,16,128]{2,1,0:T(8,128)S(1)} %copy-done.8, f32[2,4]{1,0:T(2,128)S(1)} %copy-done.6, f32[2,4,4]{2,1,0:T(4,128)S(1)} %copy-done.5, f32[2,4]{1,0:T(2,128)S(1)} %copy-done.2), custom_call_target="tpu_custom_call" | custom-call | flops 2000000000 | bytes 1048576 | tf_op jit(solution)/shard_map/middle/pallas_call | solution.py:338
  46.0 10.6 %all_to_all.21.received_ref = bf16[32,16,128]{2,1,0:T(8,128)(2,1)S(1)} all-to-all(bf16[32,16,128]{2,1,0:T(8,128)(2,1)S(1)} %get-tuple-element.20), channel_id=1, replica_groups=mesh['zlo'=2,'y'=4,'blk'=16] {'zlo','blk'}, dimensions={0} | all-to-all | bytes 262144 | tf_op jit(solution)/shard_map/all_to_all | solution.py:254
  56.7 0.0 collective-permute-done.4.refs_5_
  56.7 2.5 %feed.1 = bf16[32,16,128]{2,1,0:T(8,128)(2,1)S(1)} custom-call(bf16[32,16,128]{2,1,0:T(8,128)(2,1)S(1)} %all_to_all.21.received_ref, bf16[3,256,256]{2,1,0:T(8,128)(2,1)S(1)} %copy-done, bf16[3,256,256]{2,1,0:T(8,128)(2,1)S(1)} %collective-permute-done.refs_1_, bf16[3,256,256]{2,1,0:T(8,128)(2,1)} %collective-permute-done.1.refs_2_, ...), custom_call_target="tpu_custom_call" | custom-call | tf_op jit(solution)/shard_map/feed/pallas_call | solution.py:352
  59.2 13.4 %all_to_all.22.received_ref = bf16[32,16,128]{2,1,0:T(8,128)(2,1)} all-to-all(bf16[32,16,128]{2,1,0:T(8,128)(2,1)S(1)} %feed.1), channel_id=1, replica_groups=mesh['zlo'=2,'y'=4,'blk'=16] {'zlo','blk'}, dimensions={0} | all-to-all | bytes 262144 | tf_op jit(solution)/shard_map/all_to_all | solution.py:254
  72.6 1.6 %leave.1 = f32[1,4,2048]{2,1,0:T(4,128)} custom-call(bf16[32,16,128]{2,1,0:T(8,128)(2,1)} %all_to_all.22.received_ref, f32[4,16,128]{2,1,0:T(8,128)} %copy-done.1, f32[2,4]{1,0:T(2,128)} %depth_ref.3), custom_call_target="tpu_custom_call" | custom-call | tf_op jit(solution)/shard_map/leave/pallas_call | solution.py:367
  (18 shorter events, 0.0 us)
Async XLA Ops:
  0.0 24.4 %copy-start.7 = (s32[16]{0:T(128)S(1)}, s32[16]{0:T(128)}, u32[]{:S(2)}) copy-start(s32[16]{0:T(128)} %length_ref.1) | copy-start | bytes 196
  0.0 24.4 %copy-start.3 = (bf16[3,2048,128]{2,1,0:T(8,128)(2,1)S(1)}, bf16[3,2048,128]{2,1,0:T(8,128)(2,1)}, u32[]{:S(2)}) copy-start(bf16[3,2048,128]{2,1,0:T(8,128)(2,1)} %weight_hbm.1) | copy-start | bytes 4718596
  0.0 24.4 %copy-start.4 = (bf16[128,2048]{1,0:T(8,128)(2,1)S(1)}, bf16[128,2048]{1,0:T(8,128)(2,1)}, u32[]{:S(2)}) copy-start(bf16[128,2048]{1,0:T(8,128)(2,1)} %out_weight_hbm.1) | copy-start | bytes 1572868
  3.2 14.9 %collective-permute-start.3 = (bf16[3,256,256]{2,1,0:T(8,128)(2,1)}, bf16[3,256,256]{2,1,0:T(8,128)(2,1)}, u32[]{:S(2)}, u32[]{:S(2)}) collective-permute-start(bf16[3,256,256]{2,1,0:T(8,128)(2,1)} %get-tuple-element.25), channel_id=1, source_target_pairs={{0,64},{64,0},{1,65},{65,1},{2,66},{66,2},{3,67},{67,3},{4,68},{68... | collective-permute-start | bytes 1179656 | tf_op jit(solution)/shard_map/ppermute | solution.py:304
  5.7 15.7 %collective-permute-start = (bf16[3,256,256]{2,1,0:T(8,128)(2,1)}, bf16[3,256,256]{2,1,0:T(8,128)(2,1)S(1)}, u32[]{:S(2)}, u32[]{:S(2)}) collective-permute-start(bf16[3,256,256]{2,1,0:T(8,128)(2,1)} %get-tuple-element.21.refs_0_), channel_id=1, source_target_pairs={{16,0},{32,16},{48,32},{0,48},{17,1},{33,17},{49,33},{1,49},{18,2}... | collective-permute-start | bytes 1179656 | tf_op jit(solution)/shard_map/ppermute | solution.py:299
  8.5 15.9 %all-to-all-start = ((bf16[16,16,128]{2,1,0:T(8,128)(2,1)}), bf16[16,16,128]{2,1,0:T(8,128)(2,1)S(1)}, u32[]{:S(2)}, u32[]{:S(2)}) async-start(bf16[16,16,128]{2,1,0:T(8,128)(2,1)} %get-tuple-element.16), calls=%async_computation | async-start | bytes 131072 | tf_op jit(solution)/shard_map/all_to_all | solution.py:254
  17.0 28.0 %collective-permute-start.1 = (bf16[3,256,256]{2,1,0:T(8,128)(2,1)}, bf16[3,256,256]{2,1,0:T(8,128)(2,1)}, u32[]{:S(2)}, u32[]{:S(2)}) collective-permute-start(bf16[3,256,256]{2,1,0:T(8,128)(2,1)} %get-tuple-element.21.refs_0_), channel_id=1, source_target_pairs={{32,0},{48,16},{0,32},{16,48},{33,1},{49,17},{1,33},{17,49},{34,2}... | collective-permute-start | bytes 1179656 | tf_op jit(solution)/shard_map/ppermute | solution.py:299
  17.4 27.7 %collective-permute-start.2 = (bf16[3,256,256]{2,1,0:T(8,128)(2,1)}, bf16[3,256,256]{2,1,0:T(8,128)(2,1)}, u32[]{:S(2)}, u32[]{:S(2)}) collective-permute-start(bf16[3,256,256]{2,1,0:T(8,128)(2,1)} %get-tuple-element.21.refs_0_), channel_id=1, source_target_pairs={{48,0},{0,16},{16,32},{32,48},{49,1},{1,17},{17,33},{33,49},{50,2}... | collective-permute-start | bytes 1179656 | tf_op jit(solution)/shard_map/ppermute | solution.py:299
  18.1 38.6 %collective-permute-start.4 = (bf16[3,256,256]{2,1,0:T(8,128)(2,1)}, bf16[3,256,256]{2,1,0:T(8,128)(2,1)}, u32[]{:S(2)}, u32[]{:S(2)}) collective-permute-start(bf16[3,256,256]{2,1,0:T(8,128)(2,1)} %collective-permute-done.3.refs_4_), channel_id=1, source_target_pairs={{16,0},{32,16},{48,32},{0,48},{17,1},{33,17},{49,33},{1,49},{18,2}... | collective-permute-start | bytes 1179656 | tf_op jit(solution)/shard_map/ppermute | solution.py:299
  20.1 36.6 %collective-permute-start.5 = (bf16[3,256,256]{2,1,0:T(8,128)(2,1)}, bf16[3,256,256]{2,1,0:T(8,128)(2,1)}, u32[]{:S(2)}, u32[]{:S(2)}) collective-permute-start(bf16[3,256,256]{2,1,0:T(8,128)(2,1)} %collective-permute-done.3.refs_4_), channel_id=1, source_target_pairs={{32,0},{48,16},{0,32},{16,48},{33,1},{49,17},{1,33},{17,49},{34,2}... | collective-permute-start | bytes 1179656 | tf_op jit(solution)/shard_map/ppermute | solution.py:299
  21.5 35.2 %collective-permute-start.6 = (bf16[3,256,256]{2,1,0:T(8,128)(2,1)}, bf16[3,256,256]{2,1,0:T(8,128)(2,1)}, u32[]{:S(2)}, u32[]{:S(2)}) collective-permute-start(bf16[3,256,256]{2,1,0:T(8,128)(2,1)} %collective-permute-done.3.refs_4_), channel_id=1, source_target_pairs={{48,0},{0,16},{16,32},{32,48},{49,1},{1,17},{17,33},{33,49},{50,2}... | collective-permute-start | bytes 1179656 | tf_op jit(solution)/shard_map/ppermute | solution.py:299
  24.4 20.7 %copy-start.2 = (f32[2,4]{1,0:T(2,128)S(1)}, f32[2,4]{1,0:T(2,128)}, u32[]{:S(2)}) copy-start(f32[2,4]{1,0:T(2,128)} %depth_ref.3) | copy-start | bytes 100
  24.4 20.6 %copy-start.5 = (f32[2,4,4]{2,1,0:T(4,128)S(1)}, f32[2,4,4]{2,1,0:T(4,128)}, u32[]{:S(2)}) copy-start(f32[2,4,4]{2,1,0:T(4,128)} %mix_ref.3) | copy-start | bytes 388
  24.4 20.6 %copy-start.6 = (f32[2,4]{1,0:T(2,128)S(1)}, f32[2,4]{1,0:T(2,128)}, u32[]{:S(2)}) copy-start(f32[2,4]{1,0:T(2,128)} %width_ref.3) | copy-start | bytes 100
  24.4 20.6 %copy-start.8 = (f32[4,16,128]{2,1,0:T(8,128)S(1)}, f32[4,16,128]{2,1,0:T(8,128)}, u32[]{:S(2)}) copy-start(f32[4,16,128]{2,1,0:T(8,128)} %get-tuple-element.19.mixed_ref) | copy-start | bytes 98308
  24.5 32.2 %copy-start = (bf16[3,256,256]{2,1,0:T(8,128)(2,1)S(1)}, bf16[3,256,256]{2,1,0:T(8,128)(2,1)}, u32[]{:S(2)}) copy-start(bf16[3,256,256]{2,1,0:T(8,128)(2,1)} %get-tuple-element.21.refs_0_) | copy-start | bytes 1179652
  46.0 26.6 %copy-start.1 = (f32[4,16,128]{2,1,0:T(8,128)}, f32[4,16,128]{2,1,0:T(8,128)S(1)}, u32[]{:S(2)}) copy-start(f32[4,16,128]{2,1,0:T(8,128)S(1)} %get-tuple-element.26.base_ref) | copy-start | bytes 98308

commit v7 on v6

--- a/solution.py
+++ b/solution.py
@@ -49,9 +49,9 @@
         ]
     for copy in copies:
         copy.start()
-    streams, rows = tiles.shape[0], tiles.shape[1]
+    streams, rows = mixed_ref.shape[0], tiles.shape[1]
     for row in range(rows):
-        tiles[:, row, :] = state_ref[0, :, row * LANES : (row + 1) * LANES]
+        tiles[:streams, row, :] = state_ref[0, :, row * LANES : (row + 1) * LANES]
     state = [tiles[stream] for stream in range(streams)]
     combined = sum(width_ref[0, stream] * state[stream] for stream in range(streams))
     normed = normalize(combined).astype(send_ref.dtype)
@@ -240,10 +240,11 @@
     first = pltpu.roll(straight[:half] + crossed[half:], shift, 0)
     second = pltpu.roll(straight[half:] + crossed[:half], shift, 0)
     mlp_out = jnp.concatenate([first, second], axis=0)
-    for stream in range(tiles.shape[0]):
+    streams = base_ref.shape[0]
+    for stream in range(streams):
         tiles[stream] = base_ref[stream] + depth_ref[1, stream] * mlp_out
     for row in range(tiles.shape[1]):
-        out_ref[0, :, row * LANES : (row + 1) * LANES] = tiles[:, row, :]
+        out_ref[0, :, row * LANES : (row + 1) * LANES] = tiles[:streams, row, :]
 
 
 def cut(total, size):
@@ -289,7 +290,7 @@
         ],
         in_specs=[VMEM] + [HBM] * 3 + [SMEM] * 2,
         out_specs=[VMEM] * 4,
-        scratch_shapes=[pltpu.VMEM((streams,) + tiles, f32), pltpu.SemaphoreType.DMA((6,))],
+        scratch_shapes=[pltpu.VMEM((8 * pl.cdiv(streams, 8),) + tiles, f32), pltpu.SemaphoreType.DMA((6,))],
         cost_estimate=pl.CostEstimate(flops=30 * 10**9, transcendentals=0, bytes_accessed=2**20),
         name="enter",
     )(hyper_state, w_gate, w_up, w_down, width_in, stream_mix)
@@ -317,7 +318,7 @@
             pltpu.VMEM(attn_out_weight.shape, bf16),
             pltpu.VMEM((slots * group, head), bf16),
             pltpu.VMEM((slots * group, head), bf16),
-            pltpu.VMEM((group, slots * group), f32),
+            pltpu.VMEM((group, LANES * pl.cdiv(slots * group, LANES)), f32),
             pltpu.VMEM((group,) + tiles, f32),
             pltpu.SemaphoreType.DMA((2 + 2 * len(pieces),)),
         ],
@@ -369,7 +370,7 @@
         out_shape=jax.ShapeDtypeStruct(hyper_state.shape, f32),
         in_specs=[VMEM] * 2 + [SMEM],
         out_specs=VMEM,
-        scratch_shapes=[pltpu.VMEM((streams,) + tiles, f32)],
+        scratch_shapes=[pltpu.VMEM((8 * pl.cdiv(streams, 8),) + tiles, f32)],
         name="leave",
     )(received, base, depth_out)
 

time: 74.6 us -> 74.6 us (level)
  no operation moved by 1% of the time
where the time goes in v7:
time: 74.6 us; the launch traced here: 74.2 us
  blocking collectives  36.7 us (49%)
  starting transfers between devices  18.3 us (25%)
  Pallas kernels  16.1 us (22%)
  waiting for transfers between devices  2.94 us (4%)
    all_to_all x3, blocking collectives, exchange(): return lax.all_to_all(rows, axes, split_axis=0, concat_axis=0, tiled=True)  36.7 us
    all_to_all x1, starting transfers between devices, exchange(): return lax.all_to_all(rows, axes, split_axis=0, concat_axis=0, tiled=True)  8.57 us
    pallas_call x1, Pallas kernels, on_device(): pl.pallas_call(functools.partial(attend_kernel, pieces=pieces, steps=step...  7.97 us
    ppermute x6, starting transfers between devices, gathered(): lax.ppermute(array, 'y', [((place + distance) % ring, place) for place in...  7.17 us
    pallas_call x1, Pallas kernels, on_device(): pl.pallas_call(enter_kernel, out_shape=[jax.ShapeDtypeStruct((blk_count,)...  3.16 us
    all_to_all x1, waiting for transfers between devices, exchange(): return lax.all_to_all(rows, axes, split_axis=0, concat_axis=0, tiled=True)  2.92 us
    ppermute x1, starting transfers between devices, on_device(): far = gathered(lax.ppermute(sent, 'zlo', [(0, 1), (1, 0)]))  2.55 us
    pallas_call x1, Pallas kernels, on_device(): pl.pallas_call(feed_kernel, out_shape=jax.ShapeDtypeStruct((plane_count,)...  2.52 us
  transfers between devices with their start and end apart: 8, of which 1 were waited for; matrix products, arithmetic and copies ran while one was open for 0% of the time, Pallas kernels for 12%

profile of v7, /device:TPU:1, one launch (start us, length us, event | category | flops | bytes accessed | tf_op | source)
XLA Modules:
  0.0 74.2 jit_solution(1175079835983273011)
XLA Ops:
  0.0 3.2 %enter.1 = (bf16[16,16,128]{2,1,0:T(8,128)(2,1)}, f32[4,16,128]{2,1,0:T(8,128)}, bf16[3,256,256]{2,1,0:T(8,128)(2,1)}, bf16[3,256,256]{2,1,0:T(8,128)(2,1)}) custom-call(f32[1,4,2048]{2,1,0:T(4,128)} %state_ref.1, bf16[256,512]{1,0:T(8,128)(2,1)} %gate_hbm.1, bf16[256,512]{1,0:T(8,128)(2,1)} %up_hbm.1, bf16[512,256]{1,0:T(8,128)(2,1)} %down_hbm.1, ...), custom_call_target="tpu_custom_call" | custom-call | flops 30000001024 | bytes 1048576 | tf_op jit(solution)/shard_map/enter/pallas_call | solution.py:283
  3.2 2.5 %collective-permute-start.3 = (bf16[3,256,256]{2,1,0:T(8,128)(2,1)}, bf16[3,256,256]{2,1,0:T(8,128)(2,1)}, u32[]{:S(2)}, u32[]{:S(2)}) collective-permute-start(bf16[3,256,256]{2,1,0:T(8,128)(2,1)} %get-tuple-element.25), channel_id=1, source_target_pairs={{0,64},{64,0},{1,65},{65,1},{2,66},{66,2},{3,67},{67,3},{4,68},{68... | collective-permute-start | bytes 1179656 | tf_op jit(solution)/shard_map/ppermute | solution.py:305
  5.7 2.7 %collective-permute-start = (bf16[3,256,256]{2,1,0:T(8,128)(2,1)}, bf16[3,256,256]{2,1,0:T(8,128)(2,1)S(1)}, u32[]{:S(2)}, u32[]{:S(2)}) collective-permute-start(bf16[3,256,256]{2,1,0:T(8,128)(2,1)} %get-tuple-element.21.refs_0_), channel_id=1, source_target_pairs={{16,0},{32,16},{48,32},{0,48},{17,1},{33,17},{49,33},{1,49},{18,2}... | collective-permute-start | bytes 1179656 | tf_op jit(solution)/shard_map/ppermute | solution.py:300
  8.5 8.6 %all-to-all-start = ((bf16[16,16,128]{2,1,0:T(8,128)(2,1)}), bf16[16,16,128]{2,1,0:T(8,128)(2,1)S(1)}, u32[]{:S(2)}, u32[]{:S(2)}) async-start(bf16[16,16,128]{2,1,0:T(8,128)(2,1)} %get-tuple-element.16), calls=%async_computation | async-start | bytes 131072 | tf_op jit(solution)/shard_map/all_to_all | solution.py:255
  17.0 0.3 collective-permute-start.1
  17.4 0.7 collective-permute-start.2
  18.1 0.0 collective-permute-done.3.refs_4_
  18.1 2.0 %collective-permute-start.4 = (bf16[3,256,256]{2,1,0:T(8,128)(2,1)}, bf16[3,256,256]{2,1,0:T(8,128)(2,1)}, u32[]{:S(2)}, u32[]{:S(2)}) collective-permute-start(bf16[3,256,256]{2,1,0:T(8,128)(2,1)} %collective-permute-done.3.refs_4_), channel_id=1, source_target_pairs={{16,0},{32,16},{48,32},{0,48},{17,1},{33,17},{49,33},{1,49},{18,2}... | collective-permute-start | bytes 1179656 | tf_op jit(solution)/shard_map/ppermute | solution.py:300
  20.1 1.4 %collective-permute-start.5 = (bf16[3,256,256]{2,1,0:T(8,128)(2,1)}, bf16[3,256,256]{2,1,0:T(8,128)(2,1)}, u32[]{:S(2)}, u32[]{:S(2)}) collective-permute-start(bf16[3,256,256]{2,1,0:T(8,128)(2,1)} %collective-permute-done.3.refs_4_), channel_id=1, source_target_pairs={{32,0},{48,16},{0,32},{16,48},{33,1},{49,17},{1,33},{17,49},{34,2}... | collective-permute-start | bytes 1179656 | tf_op jit(solution)/shard_map/ppermute | solution.py:300
  21.5 0.0 collective-permute-done.refs_1_
  21.5 0.0 collective-permute-start.6
  21.5 2.9 %all-to-all-done.rows_ref = bf16[16,16,128]{2,1,0:T(8,128)(2,1)S(1)} async-done(((bf16[16,16,128]{2,1,0:T(8,128)(2,1)}), bf16[16,16,128]{2,1,0:T(8,128)(2,1)S(1)}, u32[]{:S(2)}, u32[]{:S(2)}) %all-to-all-start) | async-done | bytes 65568 | tf_op jit(solution)/shard_map/all_to_all | solution.py:255
  24.4 0.0 copy-start.2
  24.4 0.0 copy-start.5
  24.4 0.0 copy-start.6
  24.4 0.0 copy-start.8
  24.5 8.0 %attend.1 = bf16[16,16,128]{2,1,0:T(8,128)(2,1)S(1)} custom-call(bf16[16,16,128]{2,1,0:T(8,128)(2,1)S(1)} %all-to-all-done.rows_ref, s32[16]{0:T(128)S(1)} %copy-done.7, bf16[3,2048,128]{2,1,0:T(8,128)(2,1)S(1)} %copy-done.3, bf16[32832,128]{1,0:T(8,128)(2,1)} %bitcast.10, bf16[32832,128]{1,0:T(8,128)(2,1)} %bitcast.11, bf16[128,2048]{1,0:T(8,128)(2,1)S(1)} %copy-done.4), custom_call_target="tpu_custom_call" | custom-call | flops 3000000053248 | bytes 20971520 | tf_op jit(solution)/shard_map/attend/pallas_call | solution.py:311
  32.4 12.6 %all_to_all.20.received_ref = bf16[16,16,128]{2,1,0:T(8,128)(2,1)S(1)} all-to-all(bf16[16,16,128]{2,1,0:T(8,128)(2,1)S(1)} %attend.1), channel_id=1, replica_groups=mesh['zlo'=2,'y'=4,'blk'=16] {'blk'}, dimensions={0} | all-to-all | bytes 131072 | tf_op jit(solution)/shard_map/all_to_all | solution.py:255
  45.1 0.9 %middle.1 = (bf16[32,16,128]{2,1,0:T(8,128)(2,1)S(1)}, f32[4,16,128]{2,1,0:T(8,128)S(1)}) custom-call(bf16[16,16,128]{2,1,0:T(8,128)(2,1)S(1)} %all_to_all.20.received_ref, f32[4,16,128]{2,1,0:T(8,128)S(1)} %copy-done.8, f32[2,4]{1,0:T(2,128)S(1)} %copy-done.6, f32[2,4,4]{2,1,0:T(4,128)S(1)} %copy-done.5, f32[2,4]{1,0:T(2,128)S(1)} %copy-done.2), custom_call_target="tpu_custom_call" | custom-call | flops 2000000000 | bytes 1048576 | tf_op jit(solution)/shard_map/middle/pallas_call | solution.py:339
  46.0 10.6 %all_to_all.21.received_ref = bf16[32,16,128]{2,1,0:T(8,128)(2,1)S(1)} all-to-all(bf16[32,16,128]{2,1,0:T(8,128)(2,1)S(1)} %get-tuple-element.20), channel_id=1, replica_groups=mesh['zlo'=2,'y'=4,'blk'=16] {'zlo','blk'}, dimensions={0} | all-to-all | bytes 262144 | tf_op jit(solution)/shard_map/all_to_all | solution.py:255
  56.7 0.0 collective-permute-done.4.refs_5_
  56.7 2.5 %feed.1 = bf16[32,16,128]{2,1,0:T(8,128)(2,1)S(1)} custom-call(bf16[32,16,128]{2,1,0:T(8,128)(2,1)S(1)} %all_to_all.21.received_ref, bf16[3,256,256]{2,1,0:T(8,128)(2,1)S(1)} %copy-done, bf16[3,256,256]{2,1,0:T(8,128)(2,1)S(1)} %collective-permute-done.refs_1_, bf16[3,256,256]{2,1,0:T(8,128)(2,1)} %collective-permute-done.1.refs_2_, ...), custom_call_target="tpu_custom_call" | custom-call | tf_op jit(solution)/shard_map/feed/pallas_call | solution.py:353
  59.2 13.4 %all_to_all.22.received_ref = bf16[32,16,128]{2,1,0:T(8,128)(2,1)} all-to-all(bf16[32,16,128]{2,1,0:T(8,128)(2,1)S(1)} %feed.1), channel_id=1, replica_groups=mesh['zlo'=2,'y'=4,'blk'=16] {'zlo','blk'}, dimensions={0} | all-to-all | bytes 262144 | tf_op jit(solution)/shard_map/all_to_all | solution.py:255
  72.6 1.6 %leave.1 = f32[1,4,2048]{2,1,0:T(4,128)} custom-call(bf16[32,16,128]{2,1,0:T(8,128)(2,1)} %all_to_all.22.received_ref, f32[4,16,128]{2,1,0:T(8,128)} %copy-done.1, f32[2,4]{1,0:T(2,128)} %depth_ref.3), custom_call_target="tpu_custom_call" | custom-call | tf_op jit(solution)/shard_map/leave/pallas_call | solution.py:368
  (18 shorter events, 0.0 us)
Async XLA Ops:
  0.0 24.4 %copy-start.7 = (s32[16]{0:T(128)S(1)}, s32[16]{0:T(128)}, u32[]{:S(2)}) copy-start(s32[16]{0:T(128)} %length_ref.1) | copy-start | bytes 196
  0.0 24.4 %copy-start.3 = (bf16[3,2048,128]{2,1,0:T(8,128)(2,1)S(1)}, bf16[3,2048,128]{2,1,0:T(8,128)(2,1)}, u32[]{:S(2)}) copy-start(bf16[3,2048,128]{2,1,0:T(8,128)(2,1)} %weight_hbm.1) | copy-start | bytes 4718596
  0.0 24.4 %copy-start.4 = (bf16[128,2048]{1,0:T(8,128)(2,1)S(1)}, bf16[128,2048]{1,0:T(8,128)(2,1)}, u32[]{:S(2)}) copy-start(bf16[128,2048]{1,0:T(8,128)(2,1)} %out_weight_hbm.1) | copy-start | bytes 1572868
  3.2 14.9 %collective-permute-start.3 = (bf16[3,256,256]{2,1,0:T(8,128)(2,1)}, bf16[3,256,256]{2,1,0:T(8,128)(2,1)}, u32[]{:S(2)}, u32[]{:S(2)}) collective-permute-start(bf16[3,256,256]{2,1,0:T(8,128)(2,1)} %get-tuple-element.25), channel_id=1, source_target_pairs={{0,64},{64,0},{1,65},{65,1},{2,66},{66,2},{3,67},{67,3},{4,68},{68... | collective-permute-start | bytes 1179656 | tf_op jit(solution)/shard_map/ppermute | solution.py:305
  5.7 15.7 %collective-permute-start = (bf16[3,256,256]{2,1,0:T(8,128)(2,1)}, bf16[3,256,256]{2,1,0:T(8,128)(2,1)S(1)}, u32[]{:S(2)}, u32[]{:S(2)}) collective-permute-start(bf16[3,256,256]{2,1,0:T(8,128)(2,1)} %get-tuple-element.21.refs_0_), channel_id=1, source_target_pairs={{16,0},{32,16},{48,32},{0,48},{17,1},{33,17},{49,33},{1,49},{18,2}... | collective-permute-start | bytes 1179656 | tf_op jit(solution)/shard_map/ppermute | solution.py:300
  8.5 15.9 %all-to-all-start = ((bf16[16,16,128]{2,1,0:T(8,128)(2,1)}), bf16[16,16,128]{2,1,0:T(8,128)(2,1)S(1)}, u32[]{:S(2)}, u32[]{:S(2)}) async-start(bf16[16,16,128]{2,1,0:T(8,128)(2,1)} %get-tuple-element.16), calls=%async_computation | async-start | bytes 131072 | tf_op jit(solution)/shard_map/all_to_all | solution.py:255
  17.0 28.0 %collective-permute-start.1 = (bf16[3,256,256]{2,1,0:T(8,128)(2,1)}, bf16[3,256,256]{2,1,0:T(8,128)(2,1)}, u32[]{:S(2)}, u32[]{:S(2)}) collective-permute-start(bf16[3,256,256]{2,1,0:T(8,128)(2,1)} %get-tuple-element.21.refs_0_), channel_id=1, source_target_pairs={{32,0},{48,16},{0,32},{16,48},{33,1},{49,17},{1,33},{17,49},{34,2}... | collective-permute-start | bytes 1179656 | tf_op jit(solution)/shard_map/ppermute | solution.py:300
  17.4 27.7 %collective-permute-start.2 = (bf16[3,256,256]{2,1,0:T(8,128)(2,1)}, bf16[3,256,256]{2,1,0:T(8,128)(2,1)}, u32[]{:S(2)}, u32[]{:S(2)}) collective-permute-start(bf16[3,256,256]{2,1,0:T(8,128)(2,1)} %get-tuple-element.21.refs_0_), channel_id=1, source_target_pairs={{48,0},{0,16},{16,32},{32,48},{49,1},{1,17},{17,33},{33,49},{50,2}... | collective-permute-start | bytes 1179656 | tf_op jit(solution)/shard_map/ppermute | solution.py:300
  18.1 38.6 %collective-permute-start.4 = (bf16[3,256,256]{2,1,0:T(8,128)(2,1)}, bf16[3,256,256]{2,1,0:T(8,128)(2,1)}, u32[]{:S(2)}, u32[]{:S(2)}) collective-permute-start(bf16[3,256,256]{2,1,0:T(8,128)(2,1)} %collective-permute-done.3.refs_4_), channel_id=1, source_target_pairs={{16,0},{32,16},{48,32},{0,48},{17,1},{33,17},{49,33},{1,49},{18,2}... | collective-permute-start | bytes 1179656 | tf_op jit(solution)/shard_map/ppermute | solution.py:300
  20.1 36.6 %collective-permute-start.5 = (bf16[3,256,256]{2,1,0:T(8,128)(2,1)}, bf16[3,256,256]{2,1,0:T(8,128)(2,1)}, u32[]{:S(2)}, u32[]{:S(2)}) collective-permute-start(bf16[3,256,256]{2,1,0:T(8,128)(2,1)} %collective-permute-done.3.refs_4_), channel_id=1, source_target_pairs={{32,0},{48,16},{0,32},{16,48},{33,1},{49,17},{1,33},{17,49},{34,2}... | collective-permute-start | bytes 1179656 | tf_op jit(solution)/shard_map/ppermute | solution.py:300
  21.5 35.2 %collective-permute-start.6 = (bf16[3,256,256]{2,1,0:T(8,128)(2,1)}, bf16[3,256,256]{2,1,0:T(8,128)(2,1)}, u32[]{:S(2)}, u32[]{:S(2)}) collective-permute-start(bf16[3,256,256]{2,1,0:T(8,128)(2,1)} %collective-permute-done.3.refs_4_), channel_id=1, source_target_pairs={{48,0},{0,16},{16,32},{32,48},{49,1},{1,17},{17,33},{33,49},{50,2}... | collective-permute-start | bytes 1179656 | tf_op jit(solution)/shard_map/ppermute | solution.py:300
  24.4 20.7 %copy-start.2 = (f32[2,4]{1,0:T(2,128)S(1)}, f32[2,4]{1,0:T(2,128)}, u32[]{:S(2)}) copy-start(f32[2,4]{1,0:T(2,128)} %depth_ref.3) | copy-start | bytes 100
  24.4 20.6 %copy-start.5 = (f32[2,4,4]{2,1,0:T(4,128)S(1)}, f32[2,4,4]{2,1,0:T(4,128)}, u32[]{:S(2)}) copy-start(f32[2,4,4]{2,1,0:T(4,128)} %mix_ref.3) | copy-start | bytes 388
  24.4 20.6 %copy-start.6 = (f32[2,4]{1,0:T(2,128)S(1)}, f32[2,4]{1,0:T(2,128)}, u32[]{:S(2)}) copy-start(f32[2,4]{1,0:T(2,128)} %width_ref.3) | copy-start | bytes 100
  24.4 20.6 %copy-start.8 = (f32[4,16,128]{2,1,0:T(8,128)S(1)}, f32[4,16,128]{2,1,0:T(8,128)}, u32[]{:S(2)}) copy-start(f32[4,16,128]{2,1,0:T(8,128)} %get-tuple-element.19.mixed_ref) | copy-start | bytes 98308
  24.5 32.2 %copy-start = (bf16[3,256,256]{2,1,0:T(8,128)(2,1)S(1)}, bf16[3,256,256]{2,1,0:T(8,128)(2,1)}, u32[]{:S(2)}) copy-start(bf16[3,256,256]{2,1,0:T(8,128)(2,1)} %get-tuple-element.21.refs_0_) | copy-start | bytes 1179652
  46.0 26.6 %copy-start.1 = (f32[4,16,128]{2,1,0:T(8,128)}, f32[4,16,128]{2,1,0:T(8,128)S(1)}, u32[]{:S(2)}) copy-start(f32[4,16,128]{2,1,0:T(8,128)S(1)} %get-tuple-element.26.base_ref) | copy-start | bytes 98308
